TPU v7x, 32 devices: a whole 2x2x4 slice. The times are simulated.
32 devices in a mesh: vessel: 8 (over y, x, core), xsec: 4 (over z).
Axes of the slice: x: 2, y: 2, z: 4, core: 2. Of those that a mesh axis runs over, the one named last changes fastest.
Arguments:
- populations: float32 [19, 256, 2048], P(None, 'vessel', 'xsec'), may hold values from 0 to 1, as said below
- wall_flags: int32 [256, 2048], P('vessel', 'xsec'), may hold values from 0 to 1, as said below
- positions: float32 [256, 3, 128], P(('vessel', 'xsec')), may hold values from 0 to 31, as said below
- vertex_rest_shift: float32 [256, 3, 128], P(('vessel', 'xsec')), may hold values from -3 to 3
- home_brick: int32 [256, 1], P(('vessel', 'xsec')), may hold values from 0 to 3; in each aligned block of 8 rows (0 to 7, 8 to 15, ...) at most 4 rows name the same one
Outputs:
- evolved: float32 [19, 256, 2048], P(None, 'vessel', 'xsec')
- displacement: float32 [256, 3, 128], P(('vessel', 'xsec'))
Inputs may be any that keep to these rules, and one draw needn't show every extreme that they name: `home_brick`: within the 8 blocks of one device no home index occurs more than 4 times. `positions`: the first coordinate lies within 0 to 31, the second within 0 to 15, the third within 0 to 31. `wall_flags`: every cell with y = 0, y = 63, z = 0 or z = 31 is a wall. `populations`: all entries are positive.
All inputs are finite; a program needn't handle non-finite values.
Results may differ from a plain program's by a relative error of at most 0.0033.
Values sent between devices are 32-bit elements; how exact they have to be, the bound alone decides.
A program may use at most 64 MiB of HBM per device.

v0:
```python
import functools

import jax
import jax.numpy as jnp
from jax import lax
from jax.experimental import pallas as pl
from jax.experimental.pallas import tpu as pltpu
from jax.sharding import PartitionSpec as P

NZ = 32
ITERS = 2
LATTICE = [
    [0, 0, 0],
    [1, 0, 0],
    [-1, 0, 0],
    [0, 1, 0],
    [0, -1, 0],
    [0, 0, 1],
    [0, 0, -1],
    [1, 1, 0],
    [-1, -1, 0],
    [1, -1, 0],
    [-1, 1, 0],
    [1, 0, 1],
    [-1, 0, -1],
    [1, 0, -1],
    [-1, 0, 1],
    [0, 1, 1],
    [0, -1, -1],
    [0, 1, -1],
    [0, -1, 1],
]
Q = len(LATTICE)
OPPOSITE = [0, 2, 1, 4, 3, 6, 5, 8, 7, 10, 9, 12, 11, 14, 13, 16, 15, 18, 17]
WEIGHTS = [1.0 / 3.0] + [1.0 / 18.0] * 6 + [1.0 / 36.0] * 12
RELAX_TIME = 0.8
SPRING = 0.1
LANES = 128
GROUPS = LANES // NZ
MESH = pl.DeviceIdType.MESH
X_DIRS = {s: [q for q in range(Q) if LATTICE[q][0] == s] for s in (1, -1)}
Y_DIRS = {s: [q for q in range(Q) if LATTICE[q][1] == s] for s in (1, -1)}
CORNERS = [q for q in range(Q) if LATTICE[q][0] != 0 and LATTICE[q][1] != 0]


def signed_sum(terms):
    total = None
    for sign, value in terms:
        if total is None:
            total = value if sign > 0 else -value
        else:
            total = total + value if sign > 0 else total - value
    return total


def tree_sum(terms):
    while len(terms) > 1:
        terms = [
            terms[i] + terms[i + 1] if i + 1 < len(terms) else terms[i]
            for i in range(0, len(terms), 2)
        ]
    return terms[0]


def moments(fs):
    both = [fs[q] + fs[OPPOSITE[q]] for q in range(1, Q, 2)]
    flow = {q: fs[q] - fs[OPPOSITE[q]] for q in range(1, Q, 2)}
    density = tree_sum([fs[0]] + both)
    momentum = []
    for d in range(3):
        plus = tree_sum([flow[q] for q in flow if LATTICE[q][d] == 1])
        minus = [flow[q] for q in flow if LATTICE[q][d] == -1]
        momentum.append(plus - tree_sum(minus) if minus else plus)
    return density, momentum


def kernel(
    n_vessel, n_xsec, capacity, extent_x, plane,
    pop_hbm, wall_hbm, pos_hbm, shift_hbm, home_hbm, evolved_hbm, disp,
    fbuf, wall, pos, shift, home, rbuf, mom, force, vel,
    blocks, outgoing, arrived, current, ret_out, ret_in,
    xs_out, xs_in, ys_out, ys_in, cs_in,
    pop_sem, wall_sem, small_sem, out_sem, a2a_send, a2a_recv, ret_send, ret_recv, halo_send, halo_recv,
):
    v = lax.axis_index("vessel")
    h = lax.axis_index("xsec")
    v_side = {1: lax.rem(v + 1, n_vessel), -1: lax.rem(v + n_vessel - 1, n_vessel)}
    owned = pos.shape[1]
    slots = n_xsec * capacity
    extent_y = plane // NZ
    tiles = plane // LANES
    row_groups = extent_x // 8

    small_loads = [
        pltpu.make_async_copy(source, target, small_sem.at[i])
        for i, (source, target) in enumerate(
            ((pos_hbm, pos), (shift_hbm, shift), (home_hbm, home))
        )
    ]
    for copy in small_loads:
        copy.start()
    load = pltpu.make_async_copy(pop_hbm, fbuf, pop_sem)
    load.start()
    load_wall = pltpu.make_async_copy(wall_hbm, wall, wall_sem)
    load_wall.start()

    barrier = pltpu.get_barrier_semaphore()
    for d in range(1, n_xsec):
        pl.semaphore_signal(
            barrier, inc=1, device_id=(v, lax.rem(h + d, n_xsec)), device_id_type=MESH
        )
    for sx in (1, -1):
        pl.semaphore_signal(barrier, inc=1, device_id=(v_side[sx], h), device_id_type=MESH)

    has_side = {1: h < n_xsec - 1, -1: h > 0}
    for sy in (1, -1):

        @pl.when(has_side[sy])
        def _(sy=sy):
            for sx in (1, -1):
                pl.semaphore_signal(
                    barrier, inc=1, device_id=(v_side[sx], h + sy), device_id_type=MESH
                )

        @pl.when(jnp.logical_not(has_side[sy]))
        def _(sy=sy):
            side = 0 if sy == -1 else 1
            for it in range(ITERS):
                ys_in[it, side] = jnp.zeros(ys_in.shape[2:], jnp.float32)
                for k, q in enumerate(CORNERS):
                    if LATTICE[q][1] == -sy:
                        cs_in[it, k] = jnp.zeros((8, LANES), jnp.float32)

    for copy in small_loads:
        copy.wait()

    row = lax.broadcasted_iota(jnp.int32, (8, LANES), 0)
    homes = [home[0, o] for o in range(owned)]
    places = []
    for o in range(owned):
        rank = jnp.int32(0)
        for p in range(o):
            rank = rank + (homes[p] == homes[o]).astype(jnp.int32)
        places.append(homes[o] * capacity + rank)
    for o in range(owned):
        blocks[o] = jnp.where(row == 6, 1.0, 0.0)
        for c in range(3):
            start = pos[c, o:o + 1, :]
            blocks[o, c:c + 1, :] = start
            blocks[o, 3 + c:4 + c, :] = start + shift[c, o:o + 1, :]
    values = [blocks[o] for o in range(owned)]
    for s in range(slots):
        total = None
        for o in range(owned):
            term = values[o] * (places[o] == s).astype(jnp.float32)
            total = term if total is None else total + term
        outgoing[s // capacity, s % capacity] = total

    sides = has_side[1].astype(jnp.int32) + has_side[-1].astype(jnp.int32)
    pl.semaphore_wait(barrier, n_xsec + 1 + 2 * sides)

    def exchange(source, target, send, recv):
        copies = []
        for d in range(1, n_xsec):
            peer = lax.rem(h + d, n_xsec)
            copy = pltpu.make_async_remote_copy(
                src_ref=source.at[peer],
                dst_ref=target.at[h],
                send_sem=send.at[d - 1],
                recv_sem=recv.at[d - 1],
                device_id=(v, peer),
                device_id_type=MESH,
            )
            copy.start()
            copies.append(copy)
        target[h] = source[h]
        return copies

    def moments_body(step, carry):
        rows = pl.ds(pl.multiple_of((step // tiles) * 16, 16), 16)
        lanes = pl.ds(pl.multiple_of((step % tiles) * LANES, LANES), LANES)
        density, momentum = moments([fbuf[q, rows, lanes] for q in range(Q)])
        mom[0, rows, lanes] = density
        for d in range(3):
            mom[1 + d, rows, lanes] = momentum[d]
        return carry

    def velocity_body(step, carry):
        rows = pl.ds(pl.multiple_of((step // tiles) * 16, 16), 16)
        lanes = pl.ds(pl.multiple_of((step % tiles) * LANES, LANES), LANES)
        density, momentum = moments([fbuf[q, rows, lanes] for q in range(Q)])
        mom[0, rows, lanes] = density
        inverse = 1.0 / density
        for d in range(3):
            mom[1 + d, rows, lanes] = momentum[d]
            value = (momentum[d] + 0.5 * force[d, rows, lanes]) * inverse
            vel[d, rows, lanes] = value
        return carry

    def collide_body(step, carry):
        rows = pl.ds(pl.multiple_of((step // tiles) * 8, 8), 8)
        lanes = pl.ds(pl.multiple_of((step % tiles) * LANES, LANES), LANES)
        density = mom[0, rows, lanes]
        inverse = 1.0 / density
        u = [
            (mom[1 + d, rows, lanes] + RELAX_TIME * force[d, rows, lanes]) * inverse
            for d in range(3)
        ]
        square = u[0] * u[0] + u[1] * u[1] + u[2] * u[2]
        solid = wall[rows, lanes] == 1
        gain = 1.0 / RELAX_TIME
        part = density * (1.0 - 1.5 * square)
        bases = {w: (gain * w) * part for w in sorted(set(WEIGHTS))}
        twice = {w: (2.0 * gain * w) * density for w in sorted(set(WEIGHTS))}
        half = [1.5 * component for component in u]
        f0 = fbuf[0, rows, lanes]
        rbuf[0, rows, lanes] = jnp.where(solid, f0, f0 * (1.0 - gain) + bases[WEIGHTS[0]])
        for q in range(1, Q, 2):
            o = OPPOSITE[q]
            along = signed_sum(
                [(LATTICE[q][d], half[d]) for d in range(3) if LATTICE[q][d] != 0]
            )
            fq = fbuf[q, rows, lanes]
            fo = fbuf[o, rows, lanes]
            odd = twice[WEIGHTS[q]] * along
            even = bases[WEIGHTS[q]] + odd * along
            rbuf[q, rows, lanes] = jnp.where(solid, fo, fq * (1.0 - gain) + (even + odd))
            rbuf[o, rows, lanes] = jnp.where(solid, fq, fo * (1.0 - gain) + (even - odd))
        return carry

    cell_x = lax.broadcasted_iota(jnp.int32, (extent_x, LANES), 0).astype(jnp.float32)
    cell_y = lax.broadcasted_iota(jnp.int32, (max(8, extent_y), LANES), 0).astype(jnp.float32)
    cell_z = lax.broadcasted_iota(jnp.int32, (NZ, LANES), 0).astype(jnp.float32)

    def hat(coordinate, cells):
        return jnp.maximum(0.0, 1.0 - jnp.abs(coordinate - cells))

    def weights_of(s):
        now = current[s]
        fixed = arrived[s // capacity, s % capacity]
        wx = hat(now[0:1], cell_x)
        wy = hat(now[1:2], cell_y)[:extent_y]
        wz = hat(now[2:3], cell_z)
        yz = jnp.concatenate([wy[j:j + 1] * wz for j in range(extent_y)], axis=0)
        pulls = [
            SPRING * (fixed[3 + c:4 + c] - now[c:c + 1]) * fixed[6:7] for c in range(3)
        ]
        lhs = jnp.concatenate([pull * wx for pull in pulls], axis=0)
        return wx, yz.astype(jnp.bfloat16), lhs.astype(jnp.bfloat16)

    copies = exchange(outgoing, arrived, a2a_send, a2a_recv)
    load.wait()
    load_wall.wait()
    lax.fori_loop(0, (extent_x // 16) * tiles, moments_body, 0, unroll=True)
    for copy in copies:
        copy.wait()
    for s in range(slots):
        current[s] = arrived[s // capacity, s % capacity]

    depth = lax.broadcasted_iota(jnp.int32, (extent_x, plane), 1) % NZ
    first_row = lax.broadcasted_iota(jnp.int32, (8, LANES), 0) == 0
    last_row = lax.broadcasted_iota(jnp.int32, (8, LANES), 0) == 7

    def shift_x(value, step_x, edge):
        width = value.shape[1]
        rolled = pltpu.roll(value, step_x % extent_x, 0)
        index = lax.broadcasted_iota(jnp.int32, (extent_x, width), 0)
        enters = index == (0 if step_x == 1 else extent_x - 1)
        return jnp.where(enters, jnp.broadcast_to(edge, (extent_x, width)), rolled)

    last_tile = pl.ds(plane - LANES, LANES)
    first_tile = pl.ds(0, LANES)

    for it in range(ITERS):
        parts = [weights_of(s) for s in range(slots)]
        left = jnp.concatenate([part[2] for part in parts], axis=1)
        wyz = jnp.concatenate([part[1] for part in parts], axis=1)
        field = lax.dot_general(
            left, wyz, (((1,), (1,)), ((), ())), preferred_element_type=jnp.float32
        )
        for d in range(3):
            force[d] = field[d * extent_x:(d + 1) * extent_x]
        lax.fori_loop(0, row_groups * tiles, collide_body, 0, unroll=4)

        sends = []
        for k, q in enumerate(CORNERS):
            sx, sy, _ = LATTICE[q]
            copy = pltpu.make_async_remote_copy(
                src_ref=rbuf.at[
                    q,
                    pl.ds(extent_x - 8 if sx == 1 else 0, 8),
                    last_tile if sy == 1 else first_tile,
                ],
                dst_ref=cs_in.at[it, k],
                send_sem=halo_send.at[it, 4 + k],
                recv_sem=halo_recv.at[it, 4 + k],
                device_id=(v_side[sx], h + sy),
                device_id_type=MESH,
            )
            sends.append((has_side[sy], has_side[-sy], copy))
        for can_send, _, copy in sends:

            @pl.when(can_send)
            def _(copy=copy):
                copy.start()

        for side, sx in enumerate((1, -1)):
            edge = extent_x - 1 if sx == 1 else 0
            for k, q in enumerate(X_DIRS[sx]):
                xs_out[it, side, k:k + 1, :] = rbuf[q, edge:edge + 1, :]
            copy = pltpu.make_async_remote_copy(
                src_ref=xs_out.at[it, side],
                dst_ref=xs_in.at[it, side],
                send_sem=halo_send.at[it, side],
                recv_sem=halo_recv.at[it, side],
                device_id=(v_side[sx], h),
                device_id_type=MESH,
            )
            copy.start()
            sends.append((None, None, copy))
        group = lax.broadcasted_iota(jnp.int32, (extent_x, LANES), 1) // NZ
        group8 = lax.broadcasted_iota(jnp.int32, (8, LANES), 1) // NZ
        for side, sy in enumerate((1, -1)):
            tile = last_tile if sy == 1 else first_tile
            origin = LANES - NZ if sy == 1 else 0
            dirs = Y_DIRS[sy]
            packed = None
            for g in range(GROUPS):
                part = pltpu.roll(rbuf[dirs[g], :, tile], (g * NZ - origin) % LANES, 1)
                packed = part if packed is None else jnp.where(group == g, part, packed)
            ys_out[it, side, 0:extent_x, :] = packed
            packed = None
            for g in range(row_groups):
                part = pltpu.roll(
                    rbuf[dirs[GROUPS], g * 8:(g + 1) * 8, tile], (g * NZ - origin) % LANES, 1
                )
                packed = part if packed is None else jnp.where(group8 == g, part, packed)
            ys_out[it, side, extent_x:extent_x + 8, :] = packed
            copy = pltpu.make_async_remote_copy(
                src_ref=ys_out.at[it, side],
                dst_ref=ys_in.at[it, side],
                send_sem=halo_send.at[it, 2 + side],
                recv_sem=halo_recv.at[it, 2 + side],
                device_id=(v, h + sy),
                device_id_type=MESH,
            )

            @pl.when(has_side[sy])
            def _(copy=copy):
                copy.start()

            sends.append((has_side[sy], has_side[-sy], copy))
        for q in range(Q):
            step_x, step_y, step_z = LATTICE[q]
            value = rbuf[q]
            if step_x != 0:
                value = pltpu.roll(value, step_x % extent_x, 0)
            amount = step_y * NZ + step_z
            if amount != 0:
                value = pltpu.roll(value, amount % plane, 1)
            if step_z != 0:
                value = jnp.where(depth == (0 if step_z == 1 else NZ - 1), 0.0, value)
            fbuf[q] = value

        for can_send, can_receive, copy in sends:
            if can_send is None:
                copy.wait_recv()
            else:

                @pl.when(can_receive)
                def _(copy=copy):
                    copy.wait_recv()

        for q in range(Q):
            step_x, step_y, step_z = LATTICE[q]
            amount = step_y * NZ + step_z
            if step_x != 0:
                side = 0 if step_x == 1 else 1
                edge = 0 if step_x == 1 else extent_x - 1
                k = X_DIRS[step_x].index(q)
                value = xs_in[it, side, k:k + 1, :]
                if amount != 0:
                    value = pltpu.roll(
                        jnp.broadcast_to(value, (8, plane)), amount % plane, 1
                    )[0:1]
                if step_z != 0:
                    value = jnp.where(depth[0:1] == (0 if step_z == 1 else NZ - 1), 0.0, value)
                fbuf[q, edge:edge + 1, :] = value
            if step_y != 0:
                side = 0 if step_y == 1 else 1
                origin = LANES - NZ if step_y == 1 else 0
                g = Y_DIRS[step_y].index(q)
                finish = origin + amount
                if g < GROUPS:
                    halo = pltpu.roll(
                        ys_in[it, side, 0:extent_x, :], (finish - g * NZ) % LANES, 1
                    )
                else:
                    folded = ys_in[it, side, extent_x:extent_x + 8, :]
                    halo = jnp.concatenate(
                        [
                            pltpu.roll(folded, (finish - r * NZ) % LANES, 1)
                            for r in range(row_groups)
                        ],
                        axis=0,
                    )
                if step_x != 0:
                    corner = pltpu.roll(cs_in[it, CORNERS.index(q)], amount % LANES, 1)
                    halo = shift_x(halo, step_x, corner[7:8] if step_x == 1 else corner[0:1])
                lane = lax.broadcasted_iota(jnp.int32, (extent_x, LANES), 1)
                if step_z != 0:
                    halo = jnp.where(lane % NZ == (0 if step_z == 1 else NZ - 1), 0.0, halo)
                tile = first_tile if step_y == 1 else last_tile
                enters = lane < NZ if step_y == 1 else lane >= LANES - NZ
                fbuf[q, :, tile] = jnp.where(enters, halo, fbuf[q, :, tile])
        for can_send, _, copy in sends:
            if can_send is None:
                copy.wait_send()
            else:

                @pl.when(can_send)
                def _(copy=copy):
                    copy.wait_send()

        if it == ITERS - 1:
            store = pltpu.make_async_copy(fbuf, evolved_hbm, out_sem)
            store.start()
        lax.fori_loop(0, (extent_x // 16) * tiles, velocity_body, 0, unroll=True)
        flat = vel[...].reshape(3 * extent_x, plane).astype(jnp.bfloat16)
        sampled = jnp.dot(flat, wyz, preferred_element_type=jnp.float32)
        for s in range(slots):
            wx = hat(current[s, 0:1, :], cell_x)
            moves = [
                jnp.sum(
                    sampled[c * extent_x:(c + 1) * extent_x, s * LANES:(s + 1) * LANES] * wx,
                    axis=0,
                    keepdims=True,
                )
                for c in range(3)
            ]
            for c in range(3):
                current[s, c:c + 1, :] = current[s, c:c + 1, :] + moves[c]

    for s in range(slots):
        ret_out[s // capacity, s % capacity] = current[s] - arrived[s // capacity, s % capacity]
    back = exchange(ret_out, ret_in, ret_send, ret_recv)
    for copy in back:
        copy.wait()
    for o in range(owned):
        total = None
        for s in range(slots):
            term = ret_in[s // capacity, s % capacity] * (places[o] == s).astype(jnp.float32)
            total = term if total is None else total + term
        for c in range(3):
            disp[c, o:o + 1, :] = total[c:c + 1]
    store.wait()


CHUNKS = 10


def hand_over(evolved_in, moved_in, evolved, moved, held, held_moved, in_sem, out_sem):
    size = -(-Q // CHUNKS)
    pieces = [(moved_in, held_moved, moved)]
    for first in range(0, Q, size):
        part = pl.ds(first, min(size, Q - first))
        pieces.append((evolved_in.at[part], held.at[part], evolved.at[part]))
    loads = [
        pltpu.make_async_copy(source, middle, in_sem.at[i])
        for i, (source, middle, _) in enumerate(pieces)
    ]
    stores = [
        pltpu.make_async_copy(middle, target, out_sem.at[i])
        for i, (_, middle, target) in enumerate(pieces)
    ]
    for load in loads:
        load.start()
    for load, store in zip(loads, stores):
        load.wait()
        store.start()
    for store in stores:
        store.wait()


def per_device(n_vessel, n_xsec, populations, wall_flags, positions, vertex_rest_shift, home_brick):
    owned = positions.shape[0]
    capacity = max(2, 2 * owned // n_xsec)
    slots = n_xsec * capacity
    extent_x, plane = populations.shape[1:]
    f32 = jnp.float32
    peers = max(1, n_xsec - 1)
    vmem = pl.BlockSpec(memory_space=pltpu.VMEM)
    hbm = pl.BlockSpec(memory_space=pltpu.HBM)
    exchange_shape = (n_xsec, capacity, 8, LANES)
    dma = pltpu.SemaphoreType.DMA
    evolved, moved = pl.pallas_call(
        functools.partial(kernel, n_vessel, n_xsec, capacity, extent_x, plane),
        out_shape=(
            jax.ShapeDtypeStruct(populations.shape, f32),
            jax.ShapeDtypeStruct((3, owned, LANES), f32),
        ),
        in_specs=[hbm] * 5,
        out_specs=(hbm, vmem),
        scratch_shapes=[
            pltpu.VMEM((Q, extent_x, plane), f32),
            pltpu.VMEM((extent_x, plane), jnp.int32),
            pltpu.VMEM((3, owned, LANES), f32),
            pltpu.VMEM((3, owned, LANES), f32),
            pltpu.SMEM((1, owned), jnp.int32),
            pltpu.VMEM((Q, extent_x, plane), f32),
            pltpu.VMEM((4, extent_x, plane), f32),
            pltpu.VMEM((3, extent_x, plane), f32),
            pltpu.VMEM((3, extent_x, plane), f32),
            pltpu.VMEM((owned, 8, LANES), f32),
            pltpu.VMEM(exchange_shape, f32),
            pltpu.VMEM(exchange_shape, f32),
            pltpu.VMEM((slots, 8, LANES), f32),
            pltpu.VMEM(exchange_shape, f32),
            pltpu.VMEM(exchange_shape, f32),
            pltpu.VMEM((ITERS, 2, len(X_DIRS[1]), plane), f32),
            pltpu.VMEM((ITERS, 2, len(X_DIRS[1]), plane), f32),
            pltpu.VMEM((ITERS, 2, extent_x + 8, LANES), f32),
            pltpu.VMEM((ITERS, 2, extent_x + 8, LANES), f32),
            pltpu.VMEM((ITERS, len(CORNERS), 8, LANES), f32),
            dma,
            dma,
            dma((3,)),
            dma,
            dma((peers,)),
            dma((peers,)),
            dma((peers,)),
            dma((peers,)),
            dma((ITERS, 8)),
            dma((ITERS, 8)),
        ],
        compiler_params=pltpu.CompilerParams(
            collective_id=0, has_side_effects=True, vmem_limit_bytes=67043328
        ),
    )(
        populations,
        wall_flags,
        jnp.transpose(positions, (1, 0, 2)),
        jnp.transpose(vertex_rest_shift, (1, 0, 2)),
        jnp.transpose(home_brick),
    )
    evolved, moved = pl.pallas_call(
        hand_over,
        out_shape=(
            jax.ShapeDtypeStruct(evolved.shape, f32),
            jax.ShapeDtypeStruct(moved.shape, f32),
        ),
        in_specs=[hbm, hbm],
        out_specs=(hbm, hbm),
        scratch_shapes=[
            pltpu.VMEM(evolved.shape, f32),
            pltpu.VMEM(moved.shape, f32),
            dma((CHUNKS + 1,)),
            dma((CHUNKS + 1,)),
        ],
        compiler_params=pltpu.CompilerParams(vmem_limit_bytes=67043328),
    )(evolved, moved)
    return evolved, jnp.transpose(moved, (1, 0, 2))


def solution(mesh):
    in_specs = (
        P(None, "vessel", "xsec"),
        P("vessel", "xsec"),
        P(("vessel", "xsec"), None, None),
        P(("vessel", "xsec"), None, None),
        P(("vessel", "xsec"), None),
    )
    out_specs = (P(None, "vessel", "xsec"), P(("vessel", "xsec"), None, None))
    return jax.shard_map(
        functools.partial(per_device, mesh.shape["vessel"], mesh.shape["xsec"]),
        mesh=mesh,
        in_specs=in_specs,
        out_specs=out_specs,
        check_vma=False,
    )
```

profile of v0, /device:TPU:0, one launch (start us, length us, event | category | flops | bytes accessed | tf_op | source)
XLA Modules:
  0.0 26.9 jit_solution(1193547751284282450)
XLA Ops:
  0.6 24.1 %shard_map.68 = (f32[19,32,512]{2,1,0:T(8,128)}, f32[3,8,128]{2,1,0:T(8,128)}) custom-call(f32[19,32,512]{2,1,0:T(8,128)} %pop_hbm.1, s32[32,512]{1,0:T(8,128)} %wall_hbm.1, f32[3,8,128]{2,1,0:T(8,128)} %bitcast.4, f32[3,8,128]{2,1,0:T(8,128)} %bitcast.5, s32[1,8]{1,0:T(1,128)} %bitcast.6), custom_call_target="tpu_custom_call" | custom-call | tf_op jit(solution)/shard_map/pallas_call | solution.py:496
  24.7 2.2 %shard_map.69 = (f32[19,32,512]{2,1,0:T(8,128)}, f32[3,8,128]{2,1,0:T(8,128)}) custom-call(f32[19,32,512]{2,1,0:T(8,128)} %get-tuple-element.6.evolved_in, f32[3,8,128]{2,1,0:T(8,128)} %get-tuple-element.7.moved_in), custom_call_target="tpu_custom_call" | custom-call | tf_op jit(solution)/shard_map/pallas_call | solution.py:546
where the time goes:
time: 27.2 us; the launch traced here: 26.9 us
  Pallas kernels  26.3 us (97%)
  between operations  0.64 us (2%)
    pallas_call x1, Pallas kernels, per_device(): pl.pallas_call(functools.partial(kernel, n_vessel, n_xsec, capacity, exte...  24.1 us
    pallas_call x1, Pallas kernels, per_device(): pl.pallas_call(hand_over, out_shape=(jax.ShapeDtypeStruct(evolved.shape,...  2.21 us

commit v1 on v0

--- a/solution.py
+++ b/solution.py
@@ -76,11 +76,11 @@
 
 def kernel(
     n_vessel, n_xsec, capacity, extent_x, plane,
-    pop_hbm, wall_hbm, pos_hbm, shift_hbm, home_hbm, evolved_hbm, disp,
-    fbuf, wall, pos, shift, home, rbuf, mom, force, vel,
+    pop_hbm, wall_hbm, pos_hbm, shift_hbm, home_hbm, fbuf, disp,
+    wall, pos, shift, home, rbuf, mom, force, vel,
     blocks, outgoing, arrived, current, ret_out, ret_in,
     xs_out, xs_in, ys_out, ys_in, cs_in,
-    pop_sem, wall_sem, small_sem, out_sem, a2a_send, a2a_recv, ret_send, ret_recv, halo_send, halo_recv,
+    pop_sem, wall_sem, small_sem, a2a_send, a2a_recv, ret_send, ret_recv, halo_send, halo_recv,
 ):
     v = lax.axis_index("vessel")
     h = lax.axis_index("xsec")
@@ -422,9 +422,6 @@
                 def _(copy=copy):
                     copy.wait_send()
 
-        if it == ITERS - 1:
-            store = pltpu.make_async_copy(fbuf, evolved_hbm, out_sem)
-            store.start()
         lax.fori_loop(0, (extent_x // 16) * tiles, velocity_body, 0, unroll=True)
         flat = vel[...].reshape(3 * extent_x, plane).astype(jnp.bfloat16)
         sampled = jnp.dot(flat, wyz, preferred_element_type=jnp.float32)
@@ -453,30 +450,20 @@
             total = term if total is None else total + term
         for c in range(3):
             disp[c, o:o + 1, :] = total[c:c + 1]
-    store.wait()
-
-
-CHUNKS = 10
-
-
-def hand_over(evolved_in, moved_in, evolved, moved, held, held_moved, in_sem, out_sem):
+
+
+CHUNKS = 1
+
+
+def hand_over(evolved_in, moved_in, evolved, moved, out_sem):
     size = -(-Q // CHUNKS)
-    pieces = [(moved_in, held_moved, moved)]
-    for first in range(0, Q, size):
+    stores = [pltpu.make_async_copy(moved_in, moved, out_sem.at[CHUNKS])]
+    for i, first in enumerate(range(0, Q, size)):
         part = pl.ds(first, min(size, Q - first))
-        pieces.append((evolved_in.at[part], held.at[part], evolved.at[part]))
-    loads = [
-        pltpu.make_async_copy(source, middle, in_sem.at[i])
-        for i, (source, middle, _) in enumerate(pieces)
-    ]
-    stores = [
-        pltpu.make_async_copy(middle, target, out_sem.at[i])
-        for i, (_, middle, target) in enumerate(pieces)
-    ]
-    for load in loads:
-        load.start()
-    for load, store in zip(loads, stores):
-        load.wait()
+        stores.append(
+            pltpu.make_async_copy(evolved_in.at[part], evolved.at[part], out_sem.at[i])
+        )
+    for store in stores:
         store.start()
     for store in stores:
         store.wait()
@@ -496,13 +483,12 @@
     evolved, moved = pl.pallas_call(
         functools.partial(kernel, n_vessel, n_xsec, capacity, extent_x, plane),
         out_shape=(
-            jax.ShapeDtypeStruct(populations.shape, f32),
-            jax.ShapeDtypeStruct((3, owned, LANES), f32),
+            pltpu.VMEM(populations.shape, f32),
+            pltpu.VMEM((3, owned, LANES), f32),
         ),
         in_specs=[hbm] * 5,
-        out_specs=(hbm, vmem),
+        out_specs=(vmem, vmem),
         scratch_shapes=[
-            pltpu.VMEM((Q, extent_x, plane), f32),
             pltpu.VMEM((extent_x, plane), jnp.int32),
             pltpu.VMEM((3, owned, LANES), f32),
             pltpu.VMEM((3, owned, LANES), f32),
@@ -525,7 +511,6 @@
             dma,
             dma,
             dma((3,)),
-            dma,
             dma((peers,)),
             dma((peers,)),
             dma((peers,)),
@@ -534,14 +519,19 @@
             dma((ITERS, 8)),
         ],
         compiler_params=pltpu.CompilerParams(
-            collective_id=0, has_side_effects=True, vmem_limit_bytes=67043328
+            collective_id=0, has_side_effects=True, vmem_limit_bytes=40 << 20
         ),
     )(
-        populations,
-        wall_flags,
-        jnp.transpose(positions, (1, 0, 2)),
-        jnp.transpose(vertex_rest_shift, (1, 0, 2)),
-        jnp.transpose(home_brick),
+        *(
+            pltpu.with_memory_space_constraint(value, pltpu.HBM)
+            for value in (
+                populations,
+                wall_flags,
+                jnp.transpose(positions, (1, 0, 2)),
+                jnp.transpose(vertex_rest_shift, (1, 0, 2)),
+                jnp.transpose(home_brick),
+            )
+        )
     )
     evolved, moved = pl.pallas_call(
         hand_over,
@@ -549,16 +539,14 @@
             jax.ShapeDtypeStruct(evolved.shape, f32),
             jax.ShapeDtypeStruct(moved.shape, f32),
         ),
-        in_specs=[hbm, hbm],
+        in_specs=[vmem, vmem],
         out_specs=(hbm, hbm),
-        scratch_shapes=[
-            pltpu.VMEM(evolved.shape, f32),
-            pltpu.VMEM(moved.shape, f32),
-            dma((CHUNKS + 1,)),
-            dma((CHUNKS + 1,)),
-        ],
-        compiler_params=pltpu.CompilerParams(vmem_limit_bytes=67043328),
-    )(evolved, moved)
+        scratch_shapes=[dma((CHUNKS + 1,))],
+        compiler_params=pltpu.CompilerParams(vmem_limit_bytes=1 << 20),
+    )(
+        pltpu.with_memory_space_constraint(evolved, pltpu.VMEM),
+        pltpu.with_memory_space_constraint(moved, pltpu.VMEM),
+    )
     return evolved, jnp.transpose(moved, (1, 0, 2))
 
 

time: 27.2 us -> 25.2 us (0.926)
  Pallas kernels: 26.3 us -> 24.4 us
    pallas_call x1, Pallas kernels: 2.21 us -> 1.06 us  [per_device(): pl.pallas_call(hand_over, out_shape=(jax.ShapeDtypeStruct(evolved.shape,...]
    pallas_call x1, Pallas kernels: 24.1 us -> 23.3 us  [per_device(): pl.pallas_call(functools.partial(kernel, n_vessel, n_xsec, capacity, exte...]
where the time goes in v1:
time: 25.2 us; the launch traced here: 25 us
  Pallas kernels  24.4 us (97%)
  between operations  0.64 us (3%)
    pallas_call x1, Pallas kernels, per_device(): pl.pallas_call(functools.partial(kernel, n_vessel, n_xsec, capacity, exte...  23.3 us
    pallas_call x1, Pallas kernels, per_device(): pl.pallas_call(hand_over, out_shape=(jax.ShapeDtypeStruct(evolved.shape,...  1.06 us

profile of v1, /device:TPU:0, one launch (start us, length us, event | category | flops | bytes accessed | tf_op | source)
XLA Modules:
  0.0 25.0 jit_solution(6346710423560687960)
XLA Ops:
  0.6 23.3 %shard_map.68 = (f32[19,32,512]{2,1,0:T(8,128)S(1)}, f32[3,8,128]{2,1,0:T(8,128)S(1)}) custom-call(f32[19,32,512]{2,1,0:T(8,128)} %pop_hbm.1, s32[32,512]{1,0:T(8,128)} %wall_hbm.1, f32[3,8,128]{2,1,0:T(8,128)} %bitcast.4, f32[3,8,128]{2,1,0:T(8,128)} %bitcast.5, s32[1,8]{1,0:T(1,128)} %bitcast.6), custom_call_target="tpu_custom_call" | custom-call | tf_op jit(solution)/shard_map/pallas_call | solution.py:483
  23.9 1.1 %shard_map.69 = (f32[19,32,512]{2,1,0:T(8,128)}, f32[3,8,128]{2,1,0:T(8,128)}) custom-call(f32[19,32,512]{2,1,0:T(8,128)S(1)} %get-tuple-element.6.evolved_in, f32[3,8,128]{2,1,0:T(8,128)S(1)} %get-tuple-element.7.moved_in), custom_call_target="tpu_custom_call" | custom-call | tf_op jit(solution)/shard_map/pallas_call | solution.py:536

commit v2 on v1

v2 whole, which is shorter than its diff:
```python
import functools

import jax
import jax.numpy as jnp
from jax import lax
from jax.experimental import pallas as pl
from jax.experimental.pallas import tpu as pltpu
from jax.sharding import PartitionSpec as P

NZ = 32
ITERS = 2
LATTICE = [
    [0, 0, 0],
    [1, 0, 0],
    [-1, 0, 0],
    [0, 1, 0],
    [0, -1, 0],
    [0, 0, 1],
    [0, 0, -1],
    [1, 1, 0],
    [-1, -1, 0],
    [1, -1, 0],
    [-1, 1, 0],
    [1, 0, 1],
    [-1, 0, -1],
    [1, 0, -1],
    [-1, 0, 1],
    [0, 1, 1],
    [0, -1, -1],
    [0, 1, -1],
    [0, -1, 1],
]
Q = len(LATTICE)
OPPOSITE = [0, 2, 1, 4, 3, 6, 5, 8, 7, 10, 9, 12, 11, 14, 13, 16, 15, 18, 17]
WEIGHTS = [1.0 / 3.0] + [1.0 / 18.0] * 6 + [1.0 / 36.0] * 12
RELAX_TIME = 0.8
SPRING = 0.1
LANES = 128
GROUPS = LANES // NZ
FAR = -8.0
MESH = pl.DeviceIdType.MESH
X_DIRS = {s: [q for q in range(Q) if LATTICE[q][0] == s] for s in (1, -1)}
Y_DIRS = {s: [q for q in range(Q) if LATTICE[q][1] == s] for s in (1, -1)}
CORNERS = [q for q in range(Q) if LATTICE[q][0] != 0 and LATTICE[q][1] != 0]


def signed_sum(terms):
    total = None
    for sign, value in terms:
        if total is None:
            total = value if sign > 0 else -value
        else:
            total = total + value if sign > 0 else total - value
    return total


def tree_sum(terms):
    while len(terms) > 1:
        terms = [
            terms[i] + terms[i + 1] if i + 1 < len(terms) else terms[i]
            for i in range(0, len(terms), 2)
        ]
    return terms[0]


def moments(fs):
    both = [fs[q] + fs[OPPOSITE[q]] for q in range(1, Q, 2)]
    flow = {q: fs[q] - fs[OPPOSITE[q]] for q in range(1, Q, 2)}
    density = tree_sum([fs[0]] + both)
    momentum = []
    for d in range(3):
        plus = tree_sum([flow[q] for q in flow if LATTICE[q][d] == 1])
        minus = [flow[q] for q in flow if LATTICE[q][d] == -1]
        momentum.append(plus - tree_sum(minus) if minus else plus)
    return density, momentum


def peers_by_distance(h, n):
    near = jnp.minimum(h, n - 1 - h)
    toward = jnp.where(h < n - 1 - h, 1, -1)
    order = [h]
    for k in range(1, n):
        step = (k + 1) // 2
        paired = h + step if k % 2 else h - step
        order.append(jnp.where(k <= 2 * near, paired, h + toward * (k - near)))
    return order


def kernel(
    n_vessel, n_xsec, capacity, extent_x, plane,
    pop_hbm, wall_hbm, pos_hbm, shift_hbm, home_hbm, fbuf, disp,
    wall, pos, shift, home, rbuf, mom, scale, force, vel,
    outgoing, arrived, current, ret_out, ret_in, wxs, left, wyz,
    xs_out, xs_in, ys_out, ys_in, cs_in,
    pop_sem, wall_sem, small_sem, a2a_send, a2a_recv, ret_send, ret_recv, halo_send, halo_recv,
):
    v = lax.axis_index("vessel")
    h = lax.axis_index("xsec")
    v_side = {1: lax.rem(v + 1, n_vessel), -1: lax.rem(v + n_vessel - 1, n_vessel)}
    owned = pos.shape[1]
    extent_y = plane // NZ
    tiles = plane // LANES
    row_groups = extent_x // 8
    order = peers_by_distance(h, n_xsec)
    has_side = {1: h < n_xsec - 1, -1: h > 0}

    barrier = pltpu.get_barrier_semaphore()
    for k in range(n_xsec - 1, 0, -1):
        pl.semaphore_signal(barrier, inc=1, device_id=(v, order[k]), device_id_type=MESH)
    for sx in (1, -1):
        pl.semaphore_signal(barrier, inc=1, device_id=(v_side[sx], h), device_id_type=MESH)
    small_loads = [
        pltpu.make_async_copy(source, target, small_sem.at[i])
        for i, (source, target) in enumerate(
            ((pos_hbm, pos), (shift_hbm, shift), (home_hbm, home))
        )
    ]
    for copy in small_loads:
        copy.start()
    load = pltpu.make_async_copy(pop_hbm, fbuf, pop_sem)
    load.start()
    load_wall = pltpu.make_async_copy(wall_hbm, wall, wall_sem)
    load_wall.start()

    for sy in (1, -1):

        @pl.when(has_side[sy])
        def _(sy=sy):
            for sx in (1, -1):
                pl.semaphore_signal(
                    barrier, inc=1, device_id=(v_side[sx], h + sy), device_id_type=MESH
                )

        @pl.when(jnp.logical_not(has_side[sy]))
        def _(sy=sy):
            side = 0 if sy == -1 else 1
            for it in range(ITERS):
                ys_in[it, side] = jnp.zeros(ys_in.shape[2:], jnp.float32)
                for k, q in enumerate(CORNERS):
                    if LATTICE[q][1] == -sy:
                        cs_in[it, k] = jnp.zeros((8, LANES), jnp.float32)

    for copy in small_loads:
        copy.wait()

    row = lax.broadcasted_iota(jnp.int32, (8, LANES), 0)
    upper = row < 4
    slot_row = row & 3
    homes = [home[0, o] for o in range(owned)]
    ranks = []
    for o in range(owned):
        rank = jnp.int32(0)
        for p in range(o):
            rank = rank + (homes[p] == homes[o]).astype(jnp.int32)
        ranks.append(rank)

    def spread_row(value, rows=8):
        return jnp.broadcast_to(value, (rows, LANES))

    sources = []
    for c in range(3):
        sources.append([])
        for o in range(owned):
            start = spread_row(pos[c, o:o + 1, :])
            rest = start + spread_row(shift[c, o:o + 1, :])
            sources[c].append(jnp.where(upper, start, rest))
    for p in range(n_xsec):
        chosen = [slot_row == jnp.where(homes[o] == p, ranks[o], 8) for o in range(owned)]
        for c in range(3):
            total = jnp.full((8, LANES), FAR, jnp.float32)
            for o in range(owned):
                total = jnp.where(chosen[o], sources[c][o], total)
            outgoing[p, c] = total
    place = jnp.full((8, LANES), -1, jnp.int32)
    for o in range(owned):
        place = jnp.where(row == o, homes[o] * capacity + ranks[o], place)

    sides = has_side[1].astype(jnp.int32) + has_side[-1].astype(jnp.int32)
    pl.semaphore_wait(barrier, n_xsec + 1 + 2 * sides)

    def transfer(source, target, send, recv, k):
        return pltpu.make_async_remote_copy(
            src_ref=source,
            dst_ref=target.at[h],
            send_sem=send.at[k],
            recv_sem=recv.at[h],
            device_id=(v, order[k]),
            device_id_type=MESH,
        )

    def arrival(target, send, recv, k):
        return pltpu.make_async_remote_copy(
            src_ref=target.at[order[k]],
            dst_ref=target.at[order[k]],
            send_sem=send.at[k],
            recv_sem=recv.at[order[k]],
            device_id=(v, order[k]),
            device_id_type=MESH,
        )

    outbound = [
        transfer(outgoing.at[order[k]], arrived, a2a_send, a2a_recv, k)
        for k in range(n_xsec - 1, 0, -1)
    ]
    for copy in outbound:
        copy.start()
    arrived[h] = outgoing[h]

    gain = 1.0 / RELAX_TIME

    def blocks_of(height):
        return [
            (pl.ds(r, height), pl.ds(t * LANES, LANES))
            for t in range(tiles)
            for r in range(0, extent_x, height)
        ]

    def prepare():
        for rows, lanes in blocks_of(8):
            fs = [fbuf[q, rows, lanes] for q in range(Q)]
            density, momentum = moments(fs)
            solid = wall[rows, lanes] == 1
            inverse = 1.0 / density
            mom[0, rows, lanes] = jnp.where(solid, 0.0, density)
            for d in range(3):
                mom[1 + d, rows, lanes] = momentum[d] * inverse
            scale[rows, lanes] = RELAX_TIME * inverse
            for q in range(Q):
                fbuf[q, rows, lanes] = jnp.where(solid, fs[OPPOSITE[q]], (1.0 - gain) * fs[q])

    def gather_moments():
        for rows, lanes in blocks_of(8):
            density, momentum = moments([fbuf[q, rows, lanes] for q in range(Q)])
            mom[0, rows, lanes] = density
            for d in range(3):
                mom[1 + d, rows, lanes] = momentum[d]

    def find_velocity(last):
        for rows, lanes in blocks_of(16):
            density = mom[0, rows, lanes]
            inverse = 1.0 / density
            half = 0.5 * inverse
            for d in range(3):
                moved = mom[1 + d, rows, lanes] * inverse
                value = moved + half * force[d, rows, lanes]
                vel[pl.ds(d * extent_x + rows.start, 16), lanes] = value.astype(jnp.bfloat16)
                if not last:
                    mom[1 + d, rows, lanes] = moved
            if not last:
                mom[0, rows, lanes] = jnp.where(wall[rows, lanes] == 1, 0.0, density)
                scale[rows, lanes] = RELAX_TIME * inverse

    def collide(rg, t, prepared):
        rows = pl.ds(rg * 8, 8)
        lanes = pl.ds(t * LANES, LANES)
        density = mom[0, rows, lanes]
        factor = scale[rows, lanes]
        u = [mom[1 + d, rows, lanes] + factor * force[d, rows, lanes] for d in range(3)]
        square = u[0] * u[0] + u[1] * u[1] + u[2] * u[2]
        part = density * (1.0 - 1.5 * square)
        bases = {w: (gain * w) * part for w in sorted(set(WEIGHTS))}
        twice = {w: (2.0 * gain * w) * density for w in sorted(set(WEIGHTS))}
        half = [1.5 * component for component in u]
        solid = None if prepared else wall[rows, lanes] == 1

        def write(q, own, other, change):
            if prepared:
                rbuf[q, rows, lanes] = own + change
            else:
                rbuf[q, rows, lanes] = jnp.where(solid, other, own * (1.0 - gain) + change)

        f0 = fbuf[0, rows, lanes]
        write(0, f0, f0, bases[WEIGHTS[0]])
        for q in range(1, Q, 2):
            o = OPPOSITE[q]
            along = signed_sum(
                [(LATTICE[q][d], half[d]) for d in range(3) if LATTICE[q][d] != 0]
            )
            fq = fbuf[q, rows, lanes]
            fo = fbuf[o, rows, lanes]
            odd = twice[WEIGHTS[q]] * along
            even = bases[WEIGHTS[q]] + odd * along
            write(q, fq, fo, even + odd)
            write(o, fo, fq, even - odd)

    cell_x = lax.broadcasted_iota(jnp.int32, (extent_x, LANES), 0).astype(jnp.float32)
    cell_y = lax.broadcasted_iota(jnp.int32, (max(8, extent_y), LANES), 0).astype(jnp.float32)
    cell_z = lax.broadcasted_iota(jnp.int32, (NZ, LANES), 0).astype(jnp.float32)

    def hat(coordinate, cells):
        return jnp.maximum(0.0, 1.0 - jnp.abs(coordinate - cells))

    width = capacity * LANES

    def group_lanes(k):
        return pl.ds(k * width, width)

    def build(it, k, now, fixed):
        pulls = [SPRING * (fixed[c] - now[c]) for c in range(3)]
        for j in range(capacity):
            lanes = pl.ds(k * width + j * LANES, LANES)
            wx = hat(now[0][j:j + 1], cell_x)
            wy = hat(now[1][j:j + 1], cell_y)
            wz = hat(now[2][j:j + 1], cell_z)
            wxs[it, k * capacity + j] = wx
            for y in range(extent_y):
                wyz[it, y * NZ:(y + 1) * NZ, lanes] = (wy[y:y + 1] * wz).astype(jnp.bfloat16)
            for c in range(3):
                left[it, c * extent_x:(c + 1) * extent_x, lanes] = (
                    pulls[c][j:j + 1] * wx
                ).astype(jnp.bfloat16)

    def spread(it, lanes):
        return lax.dot_general(
            left[it, :, lanes],
            wyz[it, :, lanes],
            (((1,), (1,)), ((), ())),
            preferred_element_type=jnp.float32,
        )

    def add_force(field, first):
        for d in range(3):
            part = field[d * extent_x:(d + 1) * extent_x]
            force[d] = part if first else force[d] + part

    def move(it, k):
        sampled = jnp.dot(
            vel[...], wyz[it, :, group_lanes(k)], preferred_element_type=jnp.float32
        )
        result = []
        for c in range(3):
            total = current[k, c]
            for j in range(capacity):
                part = sampled[c * extent_x:(c + 1) * extent_x, j * LANES:(j + 1) * LANES]
                step = jnp.sum(part * wxs[it, k * capacity + j], axis=0, keepdims=True)
                total = jnp.where(row == j, total + step, total)
            result.append(total)
        return result

    load.wait()
    load_wall.wait()
    prepare()
    for k in range(n_xsec):
        if k > 0:
            arrival(arrived, a2a_send, a2a_recv, k).wait_recv()
        now = [arrived[order[k], c] for c in range(3)]
        for c in range(3):
            current[k, c] = now[c]
        build(0, k, now, [pltpu.roll(now[c], 4, 0) for c in range(3)])
        add_force(spread(0, group_lanes(k)), k == 0)
    for copy in outbound:
        copy.wait_send()

    depth = lax.broadcasted_iota(jnp.int32, (extent_x, plane), 1) % NZ
    lane = lax.broadcasted_iota(jnp.int32, (extent_x, LANES), 1)
    line = lax.broadcasted_iota(jnp.int32, (1, plane), 1)

    def shift_x(value, step_x, edge):
        rolled = pltpu.roll(value, step_x % extent_x, 0)
        index = lax.broadcasted_iota(jnp.int32, value.shape, 0)
        enters = index == (0 if step_x == 1 else extent_x - 1)
        return jnp.where(enters, jnp.broadcast_to(edge, value.shape), rolled)

    last_tile = pl.ds(plane - LANES, LANES)
    first_tile = pl.ds(0, LANES)

    def halo_rows(it):
        for side, sx in enumerate((1, -1)):
            found = []
            for k, q in enumerate(X_DIRS[sx]):
                _, sy, sz = LATTICE[q]
                amount = sy * NZ + sz
                value = xs_in[it, side, k:k + 1, :]
                if amount != 0:
                    value = pltpu.roll(
                        jnp.broadcast_to(value, (8, plane)), amount % plane, 1
                    )[0:1]
                if sz != 0:
                    value = jnp.where(depth[0:1] == (0 if sz == 1 else NZ - 1), 0.0, value)
                if sy != 0:
                    outside = line < NZ if sy == 1 else line >= plane - NZ
                    value = jnp.where(outside, 0.0, value)
                found.append((q, value))
            yield (0 if sx == 1 else extent_x - 1), found

    def halo_tiles(it):
        for side, sy in enumerate((1, -1)):
            origin = LANES - NZ if sy == 1 else 0
            enters = lane < NZ if sy == 1 else lane >= LANES - NZ
            found = []
            for g, q in enumerate(Y_DIRS[sy]):
                sx, _, sz = LATTICE[q]
                amount = sy * NZ + sz
                finish = origin + amount
                if g < GROUPS:
                    value = pltpu.roll(
                        ys_in[it, side, 0:extent_x, :], (finish - g * NZ) % LANES, 1
                    )
                else:
                    folded = ys_in[it, side, extent_x:extent_x + 8, :]
                    value = jnp.concatenate(
                        [
                            pltpu.roll(folded, (finish - r * NZ) % LANES, 1)
                            for r in range(row_groups)
                        ],
                        axis=0,
                    )
                if sx != 0:
                    corner = pltpu.roll(cs_in[it, CORNERS.index(q)], amount % LANES, 1)
                    value = shift_x(value, sx, corner[7:8] if sx == 1 else corner[0:1])
                keep = enters
                if sz != 0:
                    keep = jnp.logical_and(enters, lane % NZ != (0 if sz == 1 else NZ - 1))
                found.append((q, jnp.where(keep, value, 0.0)))
            yield (first_tile if sy == 1 else last_tile), found

    def add_moments(found, where):
        mom[(0, *where)] = mom[(0, *where)] + tree_sum([value for _, value in found])
        for d in range(3):
            terms = [(LATTICE[q][d], value) for q, value in found if LATTICE[q][d] != 0]
            mom[(1 + d, *where)] = mom[(1 + d, *where)] + signed_sum(
                sorted(terms, key=lambda term: -term[0])
            )

    def halo_moments(it):
        for edge, found in halo_rows(it):
            add_moments(found, (slice(edge, edge + 1), slice(None)))
        for tile, found in halo_tiles(it):
            add_moments(found, (slice(None), tile))

    def halo_populations(it):
        for edge, found in halo_rows(it):
            for q, value in found:
                fbuf[q, edge:edge + 1, :] = value
        for tile, found in halo_tiles(it):
            for q, value in found:
                fbuf[q, :, tile] = fbuf[q, :, tile] + value

    group = lax.broadcasted_iota(jnp.int32, (extent_x, LANES), 1) // NZ
    group8 = lax.broadcasted_iota(jnp.int32, (8, LANES), 1) // NZ
    edge_groups = sorted({0, row_groups - 1})
    edge_tiles = sorted({0, tiles - 1})
    stages = [[], [], [], []]
    for rg in range(row_groups):
        for t in range(tiles):
            on_x, on_y = rg in edge_groups, t in edge_tiles
            stages[0 if on_x and on_y else 1 if on_x else 2 if on_y else 3].append((rg, t))

    def corner_copies(it):
        for k, q in enumerate(CORNERS):
            sx, sy, _ = LATTICE[q]
            copy = pltpu.make_async_remote_copy(
                src_ref=rbuf.at[
                    q,
                    pl.ds(extent_x - 8 if sx == 1 else 0, 8),
                    last_tile if sy == 1 else first_tile,
                ],
                dst_ref=cs_in.at[it, k],
                send_sem=halo_send.at[it, 4 + k],
                recv_sem=halo_recv.at[it, 4 + k],
                device_id=(v_side[sx], h + sy),
                device_id_type=MESH,
            )
            yield has_side[sy], has_side[-sy], copy

    def row_copies(it):
        for side, sx in enumerate((1, -1)):
            edge = extent_x - 1 if sx == 1 else 0
            for k, q in enumerate(X_DIRS[sx]):
                xs_out[it, side, k:k + 1, :] = rbuf[q, edge:edge + 1, :]
            yield None, None, pltpu.make_async_remote_copy(
                src_ref=xs_out.at[it, side],
                dst_ref=xs_in.at[it, side],
                send_sem=halo_send.at[it, side],
                recv_sem=halo_recv.at[it, side],
                device_id=(v_side[sx], h),
                device_id_type=MESH,
            )

    def tile_copies(it):
        for side, sy in enumerate((1, -1)):
            tile = last_tile if sy == 1 else first_tile
            origin = LANES - NZ if sy == 1 else 0
            dirs = Y_DIRS[sy]
            packed = None
            for g in range(GROUPS):
                part = pltpu.roll(rbuf[dirs[g], :, tile], (g * NZ - origin) % LANES, 1)
                packed = part if packed is None else jnp.where(group == g, part, packed)
            ys_out[it, side, 0:extent_x, :] = packed
            packed = None
            for g in range(row_groups):
                part = pltpu.roll(
                    rbuf[dirs[GROUPS], g * 8:(g + 1) * 8, tile], (g * NZ - origin) % LANES, 1
                )
                packed = part if packed is None else jnp.where(group8 == g, part, packed)
            ys_out[it, side, extent_x:extent_x + 8, :] = packed
            yield has_side[sy], has_side[-sy], pltpu.make_async_remote_copy(
                src_ref=ys_out.at[it, side],
                dst_ref=ys_in.at[it, side],
                send_sem=halo_send.at[it, 2 + side],
                recv_sem=halo_recv.at[it, 2 + side],
                device_id=(v, h + sy),
                device_id_type=MESH,
            )

    def guarded(condition, action):
        if condition is None:
            action()
        else:
            pl.when(condition)(action)

    def pass_on():
        for q in range(Q):
            step_x, step_y, step_z = LATTICE[q]
            value = rbuf[q]
            if step_x != 0:
                value = pltpu.roll(value, step_x % extent_x, 0)
            amount = step_y * NZ + step_z
            if amount != 0:
                value = pltpu.roll(value, amount % plane, 1)
            if step_z != 0:
                value = jnp.where(depth == (0 if step_z == 1 else NZ - 1), 0.0, value)
            if step_y != 0:
                column = lax.broadcasted_iota(jnp.int32, (extent_x, plane), 1)
                outside = column < NZ if step_y == 1 else column >= plane - NZ
                value = jnp.where(outside, 0.0, value)
            if step_x != 0:
                index = lax.broadcasted_iota(jnp.int32, (extent_x, plane), 0)
                value = jnp.where(index == (0 if step_x == 1 else extent_x - 1), 0.0, value)
            fbuf[q] = value

    pending = []
    for it in range(ITERS):
        last = it == ITERS - 1
        sends = []
        for stage, copies_of in zip(stages, (corner_copies, row_copies, tile_copies, None)):
            for rg, t in stage:
                collide(rg, t, it == 0)
            if copies_of is not None:
                for can_send, can_receive, copy in copies_of(it):
                    guarded(can_send, copy.start)
                    sends.append((can_send, can_receive, copy))
        pass_on()
        gather_moments()
        for _, can_receive, copy in sends:
            guarded(can_receive, copy.wait_recv)
        halo_moments(it)
        if not last:
            halo_populations(it)
        find_velocity(last)
        for can_send, _, copy in sends:
            guarded(can_send, copy.wait_send)
        if not last:
            for k in range(n_xsec):
                now = move(it, k)
                for c in range(3):
                    current[k, c] = now[c]
                build(it + 1, k, now, [pltpu.roll(arrived[order[k], c], 4, 0) for c in range(3)])
            add_force(spread(it + 1, slice(None)), True)

    for k in range(n_xsec - 1, -1, -1):
        now = move(ITERS - 1, k)
        moved = [now[c] - arrived[order[k], c] for c in range(3)]
        ret_out[k, 0] = jnp.where(upper, moved[0], pltpu.roll(moved[1], 4, 0))
        ret_out[k, 1] = moved[2]
        if k > 0:
            copy = transfer(ret_out.at[k], ret_in, ret_send, ret_recv, k)
            copy.start()
            pending.append(copy)
    halo_populations(ITERS - 1)
    totals = [jnp.zeros((8, LANES), jnp.float32) for _ in range(3)]
    for k in range(n_xsec):
        if k > 0:
            arrival(ret_in, ret_send, ret_recv, k).wait_recv()
        found = [ret_out[0, i] if k == 0 else ret_in[order[k], i] for i in range(2)]
        for j in range(capacity):
            here = place == order[k] * capacity + j
            for c in range(3):
                line_index = (c * 4 + j) % 8
                value = found[c // 2][line_index:line_index + 1]
                totals[c] = jnp.where(here, spread_row(value), totals[c])
    for c in range(3):
        disp[c] = totals[c][0:owned]
    for copy in pending:
        copy.wait_send()


CHUNKS = 1


def hand_over(evolved_in, moved_in, evolved, moved, out_sem):
    size = -(-Q // CHUNKS)
    stores = [pltpu.make_async_copy(moved_in, moved, out_sem.at[CHUNKS])]
    for i, first in enumerate(range(0, Q, size)):
        part = pl.ds(first, min(size, Q - first))
        stores.append(
            pltpu.make_async_copy(evolved_in.at[part], evolved.at[part], out_sem.at[i])
        )
    for store in stores:
        store.start()
    for store in stores:
        store.wait()


def per_device(n_vessel, n_xsec, populations, wall_flags, positions, vertex_rest_shift, home_brick):
    owned = positions.shape[0]
    capacity = max(2, 2 * owned // n_xsec)
    slots = n_xsec * capacity
    extent_x, plane = populations.shape[1:]
    f32 = jnp.float32
    vmem = pl.BlockSpec(memory_space=pltpu.VMEM)
    hbm = pl.BlockSpec(memory_space=pltpu.HBM)
    dma = pltpu.SemaphoreType.DMA
    evolved, moved = pl.pallas_call(
        functools.partial(kernel, n_vessel, n_xsec, capacity, extent_x, plane),
        out_shape=(
            pltpu.VMEM(populations.shape, f32),
            pltpu.VMEM((3, owned, LANES), f32),
        ),
        in_specs=[hbm] * 5,
        out_specs=(vmem, vmem),
        scratch_shapes=[
            pltpu.VMEM((extent_x, plane), jnp.int32),
            pltpu.VMEM((3, owned, LANES), f32),
            pltpu.VMEM((3, owned, LANES), f32),
            pltpu.SMEM((1, owned), jnp.int32),
            pltpu.VMEM((Q, extent_x, plane), f32),
            pltpu.VMEM((4, extent_x, plane), f32),
            pltpu.VMEM((extent_x, plane), f32),
            pltpu.VMEM((3, extent_x, plane), f32),
            pltpu.VMEM((3 * extent_x, plane), jnp.bfloat16),
            pltpu.VMEM((n_xsec, 3, 8, LANES), f32),
            pltpu.VMEM((n_xsec, 3, 8, LANES), f32),
            pltpu.VMEM((n_xsec, 3, 8, LANES), f32),
            pltpu.VMEM((n_xsec, 2, 8, LANES), f32),
            pltpu.VMEM((n_xsec, 2, 8, LANES), f32),
            pltpu.VMEM((ITERS, slots, extent_x, LANES), f32),
            pltpu.VMEM((ITERS, 3 * extent_x, slots * LANES), jnp.bfloat16),
            pltpu.VMEM((ITERS, plane, slots * LANES), jnp.bfloat16),
            pltpu.VMEM((ITERS, 2, len(X_DIRS[1]), plane), f32),
            pltpu.VMEM((ITERS, 2, len(X_DIRS[1]), plane), f32),
            pltpu.VMEM((ITERS, 2, extent_x + 8, LANES), f32),
            pltpu.VMEM((ITERS, 2, extent_x + 8, LANES), f32),
            pltpu.VMEM((ITERS, len(CORNERS), 8, LANES), f32),
            dma,
            dma,
            dma((3,)),
            dma((n_xsec,)),
            dma((n_xsec,)),
            dma((n_xsec,)),
            dma((n_xsec,)),
            dma((ITERS, 8)),
            dma((ITERS, 8)),
        ],
        compiler_params=pltpu.CompilerParams(
            collective_id=0, has_side_effects=True, vmem_limit_bytes=40 << 20
        ),
    )(
        *(
            pltpu.with_memory_space_constraint(value, pltpu.HBM)
            for value in (
                populations,
                wall_flags,
                jnp.transpose(positions, (1, 0, 2)),
                jnp.transpose(vertex_rest_shift, (1, 0, 2)),
                jnp.transpose(home_brick),
            )
        )
    )
    evolved, moved = pl.pallas_call(
        hand_over,
        out_shape=(
            jax.ShapeDtypeStruct(evolved.shape, f32),
            jax.ShapeDtypeStruct(moved.shape, f32),
        ),
        in_specs=[vmem, vmem],
        out_specs=(hbm, hbm),
        scratch_shapes=[dma((CHUNKS + 1,))],
        compiler_params=pltpu.CompilerParams(vmem_limit_bytes=1 << 20),
    )(
        pltpu.with_memory_space_constraint(evolved, pltpu.VMEM),
        pltpu.with_memory_space_constraint(moved, pltpu.VMEM),
    )
    return evolved, jnp.transpose(moved, (1, 0, 2))


def solution(mesh):
    in_specs = (
        P(None, "vessel", "xsec"),
        P("vessel", "xsec"),
        P(("vessel", "xsec"), None, None),
        P(("vessel", "xsec"), None, None),
        P(("vessel", "xsec"), None),
    )
    out_specs = (P(None, "vessel", "xsec"), P(("vessel", "xsec"), None, None))
    return jax.shard_map(
        functools.partial(per_device, mesh.shape["vessel"], mesh.shape["xsec"]),
        mesh=mesh,
        in_specs=in_specs,
        out_specs=out_specs,
        check_vma=False,
    )
```

time: 25.2 us -> 23.8 us (0.944)
  Pallas kernels: 24.4 us -> 23 us
    pallas_call x1, Pallas kernels: 23.3 us -> 21.9 us  [per_device(): pl.pallas_call(functools.partial(kernel, n_vessel, n_xsec, capacity, exte...]
where the time goes in v2:
time: 23.8 us; the launch traced here: 23.6 us
  Pallas kernels  23 us (97%)
  between operations  0.64 us (3%)
    pallas_call x1, Pallas kernels, per_device(): pl.pallas_call(functools.partial(kernel, n_vessel, n_xsec, capacity, exte...  21.9 us
    pallas_call x1, Pallas kernels, per_device(): pl.pallas_call(hand_over, out_shape=(jax.ShapeDtypeStruct(evolved.shape,...  1.06 us

profile of v2, /device:TPU:0, one launch (start us, length us, event | category | flops | bytes accessed | tf_op | source)
XLA Modules:
  0.0 23.6 jit_solution(5988752672857991875)
XLA Ops:
  0.6 21.9 %shard_map.68 = (f32[19,32,512]{2,1,0:T(8,128)S(1)}, f32[3,8,128]{2,1,0:T(8,128)S(1)}) custom-call(f32[19,32,512]{2,1,0:T(8,128)} %pop_hbm.1, s32[32,512]{1,0:T(8,128)} %wall_hbm.1, f32[3,8,128]{2,1,0:T(8,128)} %bitcast.4, f32[3,8,128]{2,1,0:T(8,128)} %bitcast.5, s32[1,8]{1,0:T(1,128)} %bitcast.6), custom_call_target="tpu_custom_call" | custom-call | tf_op jit(solution)/shard_map/pallas_call | solution.py:614
  22.5 1.1 %shard_map.69 = (f32[19,32,512]{2,1,0:T(8,128)}, f32[3,8,128]{2,1,0:T(8,128)}) custom-call(f32[19,32,512]{2,1,0:T(8,128)S(1)} %get-tuple-element.6.evolved_in, f32[3,8,128]{2,1,0:T(8,128)S(1)} %get-tuple-element.7.moved_in), custom_call_target="tpu_custom_call" | custom-call | tf_op jit(solution)/shard_map/pallas_call | solution.py:670

commit v3 on v2

--- a/solution.py
+++ b/solution.py
@@ -89,15 +89,16 @@
 def kernel(
     n_vessel, n_xsec, capacity, extent_x, plane,
     pop_hbm, wall_hbm, pos_hbm, shift_hbm, home_hbm, fbuf, disp,
-    wall, pos, shift, home, rbuf, mom, scale, force, vel,
-    outgoing, arrived, current, ret_out, ret_in, wxs, left, wyz,
+    wall, points, home, rbuf, mom, scale, force, vel,
+    outgoing, arrived, current, ret_out, ret_in, wxs,
     xs_out, xs_in, ys_out, ys_in, cs_in,
-    pop_sem, wall_sem, small_sem, a2a_send, a2a_recv, ret_send, ret_recv, halo_send, halo_recv,
+    load_sem, out_sem, a2a_recv, ret_recv, halo_send, halo_recv,
 ):
     v = lax.axis_index("vessel")
     h = lax.axis_index("xsec")
     v_side = {1: lax.rem(v + 1, n_vessel), -1: lax.rem(v + n_vessel - 1, n_vessel)}
-    owned = pos.shape[1]
+    owned = points.shape[2]
+    pos, shift = points.at[0], points.at[1]
     extent_y = plane // NZ
     tiles = plane // LANES
     row_groups = extent_x // 8
@@ -110,16 +111,14 @@
     for sx in (1, -1):
         pl.semaphore_signal(barrier, inc=1, device_id=(v_side[sx], h), device_id_type=MESH)
     small_loads = [
-        pltpu.make_async_copy(source, target, small_sem.at[i])
-        for i, (source, target) in enumerate(
-            ((pos_hbm, pos), (shift_hbm, shift), (home_hbm, home))
-        )
+        pltpu.make_async_copy(source, target, load_sem.at[i])
+        for i, source, target in ((0, pos_hbm, pos), (0, shift_hbm, shift), (1, home_hbm, home))
     ]
     for copy in small_loads:
         copy.start()
-    load = pltpu.make_async_copy(pop_hbm, fbuf, pop_sem)
+    load = pltpu.make_async_copy(pop_hbm, fbuf, load_sem.at[2])
     load.start()
-    load_wall = pltpu.make_async_copy(wall_hbm, wall, wall_sem)
+    load_wall = pltpu.make_async_copy(wall_hbm, wall, load_sem.at[3])
     load_wall.start()
 
     for sy in (1, -1):
@@ -140,12 +139,12 @@
                     if LATTICE[q][1] == -sy:
                         cs_in[it, k] = jnp.zeros((8, LANES), jnp.float32)
 
-    for copy in small_loads:
-        copy.wait()
+    pltpu.make_async_copy(points, points, load_sem.at[0]).wait()
+    small_loads[2].wait()
 
     row = lax.broadcasted_iota(jnp.int32, (8, LANES), 0)
-    upper = row < 4
-    slot_row = row & 3
+    odd_row = (row & 1) == 1
+    slot_row = row >> 1
     homes = [home[0, o] for o in range(owned)]
     ranks = []
     for o in range(owned):
@@ -163,7 +162,7 @@
         for o in range(owned):
             start = spread_row(pos[c, o:o + 1, :])
             rest = start + spread_row(shift[c, o:o + 1, :])
-            sources[c].append(jnp.where(upper, start, rest))
+            sources[c].append(jnp.where(odd_row, start, rest))
     for p in range(n_xsec):
         chosen = [slot_row == jnp.where(homes[o] == p, ranks[o], 8) for o in range(owned)]
         for c in range(3):
@@ -178,12 +177,15 @@
     sides = has_side[1].astype(jnp.int32) + has_side[-1].astype(jnp.int32)
     pl.semaphore_wait(barrier, n_xsec + 1 + 2 * sides)
 
+    def slot_of(sender, receiver):
+        return lax.rem(sender - receiver + n_xsec - 1, n_xsec)
+
     def transfer(source, target, send, recv, k):
         return pltpu.make_async_remote_copy(
             src_ref=source,
             dst_ref=target.at[h],
-            send_sem=send.at[k],
-            recv_sem=recv.at[h],
+            send_sem=send,
+            recv_sem=recv.at[slot_of(h, order[k])],
             device_id=(v, order[k]),
             device_id_type=MESH,
         )
@@ -192,14 +194,14 @@
         return pltpu.make_async_remote_copy(
             src_ref=target.at[order[k]],
             dst_ref=target.at[order[k]],
-            send_sem=send.at[k],
-            recv_sem=recv.at[order[k]],
+            send_sem=send,
+            recv_sem=recv.at[slot_of(order[k], h)],
             device_id=(v, order[k]),
             device_id_type=MESH,
         )
 
     outbound = [
-        transfer(outgoing.at[order[k]], arrived, a2a_send, a2a_recv, k)
+        transfer(outgoing.at[order[k]], arrived, out_sem.at[0], a2a_recv, k)
         for k in range(n_xsec - 1, 0, -1)
     ]
     for copy in outbound:
@@ -243,7 +245,9 @@
             for d in range(3):
                 moved = mom[1 + d, rows, lanes] * inverse
                 value = moved + half * force[d, rows, lanes]
-                vel[pl.ds(d * extent_x + rows.start, 16), lanes] = value.astype(jnp.bfloat16)
+                vel[lanes.start // LANES, pl.ds(d * extent_x + rows.start, 16)] = value.astype(
+                    jnp.bfloat16
+                )
                 if not last:
                     mom[1 + d, rows, lanes] = moved
             if not last:
@@ -261,6 +265,7 @@
         bases = {w: (gain * w) * part for w in sorted(set(WEIGHTS))}
         twice = {w: (2.0 * gain * w) * density for w in sorted(set(WEIGHTS))}
         half = [1.5 * component for component in u]
+
         solid = None if prepared else wall[rows, lanes] == 1
 
         def write(q, own, other, change):
@@ -290,66 +295,77 @@
     def hat(coordinate, cells):
         return jnp.maximum(0.0, 1.0 - jnp.abs(coordinate - cells))
 
-    width = capacity * LANES
-
-    def group_lanes(k):
-        return pl.ds(k * width, width)
-
     def build(it, k, now, fixed):
         pulls = [SPRING * (fixed[c] - now[c]) for c in range(3)]
+        sides, planes = [], []
         for j in range(capacity):
-            lanes = pl.ds(k * width + j * LANES, LANES)
-            wx = hat(now[0][j:j + 1], cell_x)
-            wy = hat(now[1][j:j + 1], cell_y)
-            wz = hat(now[2][j:j + 1], cell_z)
+            at = slice(2 * j + 1, 2 * j + 2)
+            wx = hat(now[0][at], cell_x)
+            wy = hat(now[1][at], cell_y)
+            wz = hat(now[2][at], cell_z)
             wxs[it, k * capacity + j] = wx
-            for y in range(extent_y):
-                wyz[it, y * NZ:(y + 1) * NZ, lanes] = (wy[y:y + 1] * wz).astype(jnp.bfloat16)
-            for c in range(3):
-                left[it, c * extent_x:(c + 1) * extent_x, lanes] = (
-                    pulls[c][j:j + 1] * wx
-                ).astype(jnp.bfloat16)
-
-    def spread(it, lanes):
+            flat = jnp.concatenate([wy[y:y + 1] * wz for y in range(extent_y)], axis=0)
+            planes.append(flat.astype(jnp.bfloat16))
+            side = jnp.concatenate([pulls[c][at] * wx for c in range(3)], axis=0)
+            sides.append(side.astype(jnp.bfloat16))
+        return jnp.concatenate(sides, axis=1), jnp.concatenate(planes, axis=1)
+
+    def spread(sides, planes):
         return lax.dot_general(
-            left[it, :, lanes],
-            wyz[it, :, lanes],
-            (((1,), (1,)), ((), ())),
-            preferred_element_type=jnp.float32,
+            sides, planes, (((1,), (1,)), ((), ())), preferred_element_type=jnp.float32
         )
+
+    def spread_t(sides, planes):
+        field = lax.dot_general(
+            planes, sides, (((1,), (1,)), ((), ())), preferred_element_type=jnp.float32
+        )
+        field = jnp.concatenate([field, jnp.zeros((plane, LANES - 3 * extent_x), jnp.float32)], axis=1)
+        return jnp.transpose(field)[0:3 * extent_x]
 
     def add_force(field, first):
         for d in range(3):
             part = field[d * extent_x:(d + 1) * extent_x]
             force[d] = part if first else force[d] + part
 
-    def move(it, k):
-        sampled = jnp.dot(
-            vel[...], wyz[it, :, group_lanes(k)], preferred_element_type=jnp.float32
-        )
+    low_rows = row < 4
+    mid_rows = jnp.logical_and(row >= 2, row < 6)
+    second = (row & 2) != 0
+
+    def merge(mask, a, b, shift):
+        return jnp.where(mask, a, b) + pltpu.roll(jnp.where(mask, b, a), shift, 0)
+
+    def row_sums(parts):
+        parts = parts + [jnp.zeros((8, LANES), jnp.float32)] * (4 - len(parts))
+        pairs = merge(low_rows, parts[1], parts[3], 4), merge(mid_rows, parts[2], parts[0], 4)
+        total = merge(second, pairs[0], pairs[1], 2)
+        return total + pltpu.roll(total, 1, 0)
+
+    def move(it, k, planes):
+        flow = jnp.concatenate([vel[t] for t in range(tiles)], axis=1)
+        sampled = jnp.dot(flow, planes, preferred_element_type=jnp.float32)
         result = []
         for c in range(3):
-            total = current[k, c]
+            parts = []
             for j in range(capacity):
                 part = sampled[c * extent_x:(c + 1) * extent_x, j * LANES:(j + 1) * LANES]
-                step = jnp.sum(part * wxs[it, k * capacity + j], axis=0, keepdims=True)
-                total = jnp.where(row == j, total + step, total)
-            result.append(total)
+                part = part * wxs[it, k * capacity + j]
+                parts.append(tree_sum([part[i:i + 8] for i in range(0, extent_x, 8)]))
+            result.append(current[k, c] + row_sums(parts))
         return result
 
     load.wait()
     load_wall.wait()
     prepare()
+    planes = []
     for k in range(n_xsec):
         if k > 0:
-            arrival(arrived, a2a_send, a2a_recv, k).wait_recv()
+            arrival(arrived, out_sem.at[0], a2a_recv, k).wait_recv()
         now = [arrived[order[k], c] for c in range(3)]
         for c in range(3):
             current[k, c] = now[c]
-        build(0, k, now, [pltpu.roll(now[c], 4, 0) for c in range(3)])
-        add_force(spread(0, group_lanes(k)), k == 0)
-    for copy in outbound:
-        copy.wait_send()
+        sides, flat = build(0, k, now, [pltpu.roll(now[c], 1, 0) for c in range(3)])
+        planes.append(flat)
+        add_force(spread(sides, flat), k == 0)
 
     depth = lax.broadcasted_iota(jnp.int32, (extent_x, plane), 1) % NZ
     lane = lax.broadcasted_iota(jnp.int32, (extent_x, LANES), 1)
@@ -422,33 +438,44 @@
                 sorted(terms, key=lambda term: -term[0])
             )
 
-    def halo_moments(it):
-        for edge, found in halo_rows(it):
+    def halo_values(it):
+        return list(halo_rows(it)), list(halo_tiles(it))
+
+    def halo_moments(values):
+        for edge, found in values[0]:
             add_moments(found, (slice(edge, edge + 1), slice(None)))
-        for tile, found in halo_tiles(it):
+        for tile, found in values[1]:
             add_moments(found, (slice(None), tile))
 
-    def halo_populations(it):
-        for edge, found in halo_rows(it):
+    def halo_populations(values):
+        for edge, found in values[0]:
             for q, value in found:
                 fbuf[q, edge:edge + 1, :] = value
-        for tile, found in halo_tiles(it):
+        for tile, found in values[1]:
             for q, value in found:
                 fbuf[q, :, tile] = fbuf[q, :, tile] + value
 
     group = lax.broadcasted_iota(jnp.int32, (extent_x, LANES), 1) // NZ
     group8 = lax.broadcasted_iota(jnp.int32, (8, LANES), 1) // NZ
     edge_groups = sorted({0, row_groups - 1})
-    edge_tiles = sorted({0, tiles - 1})
-    stages = [[], [], [], []]
+    side_tiles = {1: tiles - 1, -1: 0}
+    stages = {1: [], -1: [], 0: [], None: []}
     for rg in range(row_groups):
         for t in range(tiles):
-            on_x, on_y = rg in edge_groups, t in edge_tiles
-            stages[0 if on_x and on_y else 1 if on_x else 2 if on_y else 3].append((rg, t))
-
-    def corner_copies(it):
+            if t == side_tiles[1]:
+                stages[1].append((rg, t))
+            elif t == side_tiles[-1]:
+                stages[-1].append((rg, t))
+            elif rg in edge_groups:
+                stages[0].append((rg, t))
+            else:
+                stages[None].append((rg, t))
+
+    def corner_copies(it, side):
         for k, q in enumerate(CORNERS):
             sx, sy, _ = LATTICE[q]
+            if sy != side:
+                continue
             copy = pltpu.make_async_remote_copy(
                 src_ref=rbuf.at[
                     q,
@@ -456,29 +483,29 @@
                     last_tile if sy == 1 else first_tile,
                 ],
                 dst_ref=cs_in.at[it, k],
-                send_sem=halo_send.at[it, 4 + k],
-                recv_sem=halo_recv.at[it, 4 + k],
+                send_sem=halo_send.at[it, 2],
+                recv_sem=halo_recv.at[it, 2],
                 device_id=(v_side[sx], h + sy),
                 device_id_type=MESH,
             )
-            yield has_side[sy], has_side[-sy], copy
+            yield has_side[sy], copy
 
     def row_copies(it):
         for side, sx in enumerate((1, -1)):
             edge = extent_x - 1 if sx == 1 else 0
             for k, q in enumerate(X_DIRS[sx]):
                 xs_out[it, side, k:k + 1, :] = rbuf[q, edge:edge + 1, :]
-            yield None, None, pltpu.make_async_remote_copy(
+            yield None, pltpu.make_async_remote_copy(
                 src_ref=xs_out.at[it, side],
                 dst_ref=xs_in.at[it, side],
-                send_sem=halo_send.at[it, side],
-                recv_sem=halo_recv.at[it, side],
+                send_sem=halo_send.at[it, 0],
+                recv_sem=halo_recv.at[it, 0],
                 device_id=(v_side[sx], h),
                 device_id_type=MESH,
             )
 
-    def tile_copies(it):
-        for side, sy in enumerate((1, -1)):
+    def tile_copies(it, sy):
+        for side in (0,) if sy == 1 else (1,):
             tile = last_tile if sy == 1 else first_tile
             origin = LANES - NZ if sy == 1 else 0
             dirs = Y_DIRS[sy]
@@ -494,20 +521,34 @@
                 )
                 packed = part if packed is None else jnp.where(group8 == g, part, packed)
             ys_out[it, side, extent_x:extent_x + 8, :] = packed
-            yield has_side[sy], has_side[-sy], pltpu.make_async_remote_copy(
+            yield has_side[sy], pltpu.make_async_remote_copy(
                 src_ref=ys_out.at[it, side],
                 dst_ref=ys_in.at[it, side],
-                send_sem=halo_send.at[it, 2 + side],
-                recv_sem=halo_recv.at[it, 2 + side],
+                send_sem=halo_send.at[it, 1],
+                recv_sem=halo_recv.at[it, 1],
                 device_id=(v, h + sy),
                 device_id_type=MESH,
             )
 
-    def guarded(condition, action):
-        if condition is None:
-            action()
-        else:
-            pl.when(condition)(action)
+    def settle(it, sent):
+        def wait(kind, ref):
+            copy = pltpu.make_async_remote_copy(
+                src_ref=ref,
+                dst_ref=ref,
+                send_sem=halo_send.at[it, kind],
+                recv_sem=halo_recv.at[it, kind],
+                device_id=(v_side[1], h),
+                device_id_type=MESH,
+            )
+            return copy.wait_send if sent else copy.wait_recv
+
+        between = jnp.logical_and(has_side[1], has_side[-1])
+        half = len(CORNERS) // 2
+        pl.when(between)(wait(2, cs_in.at[it]))
+        pl.when(jnp.logical_not(between))(wait(2, cs_in.at[it, pl.ds(0, half)]))
+        pl.when(between)(wait(1, ys_in.at[it]))
+        pl.when(jnp.logical_not(between))(wait(1, ys_in.at[it, pl.ds(0, 1)]))
+        wait(0, xs_in.at[it])()
 
     def pass_on():
         for q in range(Q):
@@ -529,60 +570,78 @@
                 value = jnp.where(index == (0 if step_x == 1 else extent_x - 1), 0.0, value)
             fbuf[q] = value
 
-    pending = []
     for it in range(ITERS):
         last = it == ITERS - 1
-        sends = []
-        for stage, copies_of in zip(stages, (corner_copies, row_copies, tile_copies, None)):
-            for rg, t in stage:
+
+        def send(found):
+            for can_send, copy in found:
+                if can_send is None:
+                    copy.start()
+                else:
+                    pl.when(can_send)(copy.start)
+
+        for sy in (1, -1):
+            for rg, t in stages[sy]:
                 collide(rg, t, it == 0)
-            if copies_of is not None:
-                for can_send, can_receive, copy in copies_of(it):
-                    guarded(can_send, copy.start)
-                    sends.append((can_send, can_receive, copy))
+            send(corner_copies(it, sy))
+            send(tile_copies(it, sy))
+        for rg, t in stages[0]:
+            collide(rg, t, it == 0)
+        send(row_copies(it))
+        for rg, t in stages[None]:
+            collide(rg, t, it == 0)
         pass_on()
         gather_moments()
-        for _, can_receive, copy in sends:
-            guarded(can_receive, copy.wait_recv)
-        halo_moments(it)
+        settle(it, False)
+        values = halo_values(it)
+        halo_moments(values)
+        find_velocity(last)
         if not last:
-            halo_populations(it)
-        find_velocity(last)
-        for can_send, _, copy in sends:
-            guarded(can_send, copy.wait_send)
+            halo_populations(values)
         if not last:
+            built = []
             for k in range(n_xsec):
-                now = move(it, k)
+                now = move(it, k, planes[k])
                 for c in range(3):
                     current[k, c] = now[c]
-                build(it + 1, k, now, [pltpu.roll(arrived[order[k], c], 4, 0) for c in range(3)])
-            add_force(spread(it + 1, slice(None)), True)
+                built.append(
+                    build(it + 1, k, now, [pltpu.roll(arrived[order[k], c], 1, 0) for c in range(3)])
+                )
+            planes = [flat for _, flat in built]
+            add_force(
+                spread(
+                    jnp.concatenate([sides for sides, _ in built], axis=1),
+                    jnp.concatenate(planes, axis=1),
+                ),
+                True,
+            )
+            settle(it, True)
 
     for k in range(n_xsec - 1, -1, -1):
-        now = move(ITERS - 1, k)
+        now = move(ITERS - 1, k, planes[k])
         moved = [now[c] - arrived[order[k], c] for c in range(3)]
-        ret_out[k, 0] = jnp.where(upper, moved[0], pltpu.roll(moved[1], 4, 0))
+        ret_out[k, 0] = jnp.where(odd_row, moved[0], pltpu.roll(moved[1], 7, 0))
         ret_out[k, 1] = moved[2]
         if k > 0:
-            copy = transfer(ret_out.at[k], ret_in, ret_send, ret_recv, k)
-            copy.start()
-            pending.append(copy)
-    halo_populations(ITERS - 1)
+            transfer(ret_out.at[k], ret_in, out_sem.at[1], ret_recv, k).start()
+    halo_populations(halo_values(ITERS - 1))
     totals = [jnp.zeros((8, LANES), jnp.float32) for _ in range(3)]
     for k in range(n_xsec):
         if k > 0:
-            arrival(ret_in, ret_send, ret_recv, k).wait_recv()
+            arrival(ret_in, out_sem.at[1], ret_recv, k).wait_recv()
         found = [ret_out[0, i] if k == 0 else ret_in[order[k], i] for i in range(2)]
         for j in range(capacity):
             here = place == order[k] * capacity + j
             for c in range(3):
-                line_index = (c * 4 + j) % 8
-                value = found[c // 2][line_index:line_index + 1]
+                at = 2 * j + (0 if c == 1 else 1)
+                value = found[c // 2][at:at + 1]
                 totals[c] = jnp.where(here, spread_row(value), totals[c])
     for c in range(3):
         disp[c] = totals[c][0:owned]
-    for copy in pending:
-        copy.wait_send()
+    for i, ref in enumerate((outgoing, ret_out)):
+        whole = ref.at[pl.ds(0, n_xsec - 1)]
+        pltpu.make_async_copy(whole, whole, out_sem.at[i]).wait()
+    settle(ITERS - 1, True)
 
 
 CHUNKS = 1
@@ -621,36 +680,30 @@
         out_specs=(vmem, vmem),
         scratch_shapes=[
             pltpu.VMEM((extent_x, plane), jnp.int32),
-            pltpu.VMEM((3, owned, LANES), f32),
-            pltpu.VMEM((3, owned, LANES), f32),
+            pltpu.VMEM((2, 3, owned, LANES), f32),
             pltpu.SMEM((1, owned), jnp.int32),
             pltpu.VMEM((Q, extent_x, plane), f32),
             pltpu.VMEM((4, extent_x, plane), f32),
             pltpu.VMEM((extent_x, plane), f32),
             pltpu.VMEM((3, extent_x, plane), f32),
-            pltpu.VMEM((3 * extent_x, plane), jnp.bfloat16),
+            pltpu.VMEM((plane // LANES, 3 * extent_x, LANES), jnp.bfloat16),
             pltpu.VMEM((n_xsec, 3, 8, LANES), f32),
             pltpu.VMEM((n_xsec, 3, 8, LANES), f32),
             pltpu.VMEM((n_xsec, 3, 8, LANES), f32),
             pltpu.VMEM((n_xsec, 2, 8, LANES), f32),
             pltpu.VMEM((n_xsec, 2, 8, LANES), f32),
             pltpu.VMEM((ITERS, slots, extent_x, LANES), f32),
-            pltpu.VMEM((ITERS, 3 * extent_x, slots * LANES), jnp.bfloat16),
-            pltpu.VMEM((ITERS, plane, slots * LANES), jnp.bfloat16),
             pltpu.VMEM((ITERS, 2, len(X_DIRS[1]), plane), f32),
             pltpu.VMEM((ITERS, 2, len(X_DIRS[1]), plane), f32),
             pltpu.VMEM((ITERS, 2, extent_x + 8, LANES), f32),
             pltpu.VMEM((ITERS, 2, extent_x + 8, LANES), f32),
             pltpu.VMEM((ITERS, len(CORNERS), 8, LANES), f32),
-            dma,
-            dma,
-            dma((3,)),
-            dma((n_xsec,)),
-            dma((n_xsec,)),
-            dma((n_xsec,)),
-            dma((n_xsec,)),
-            dma((ITERS, 8)),
-            dma((ITERS, 8)),
+            dma((4,)),
+            dma((2,)),
+            dma((n_xsec - 1,)),
+            dma((n_xsec - 1,)),
+            dma((ITERS, 3)),
+            dma((ITERS, 3)),
         ],
         compiler_params=pltpu.CompilerParams(
             collective_id=0, has_side_effects=True, vmem_limit_bytes=40 << 20

time: 23.8 us -> 23 us (0.966)
  Pallas kernels: 23 us -> 22.1 us
    pallas_call x1, Pallas kernels: 21.9 us -> 21 us  [per_device(): pl.pallas_call(functools.partial(kernel, n_vessel, n_xsec, capacity, exte...]
where the time goes in v3:
time: 23 us; the launch traced here: 22.7 us
  Pallas kernels  22.1 us (96%)
  between operations  0.64 us (3%)
    pallas_call x1, Pallas kernels, per_device(): pl.pallas_call(functools.partial(kernel, n_vessel, n_xsec, capacity, exte...  21 us
    pallas_call x1, Pallas kernels, per_device(): pl.pallas_call(hand_over, out_shape=(jax.ShapeDtypeStruct(evolved.shape,...  1.06 us

profile of v3, /device:TPU:0, one launch (start us, length us, event | category | flops | bytes accessed | tf_op | source)
XLA Modules:
  0.0 22.7 jit_solution(6100964260383688227)
XLA Ops:
  0.6 21.0 %shard_map.68 = (f32[19,32,512]{2,1,0:T(8,128)S(1)}, f32[3,8,128]{2,1,0:T(8,128)S(1)}) custom-call(f32[19,32,512]{2,1,0:T(8,128)} %pop_hbm.1, s32[32,512]{1,0:T(8,128)} %wall_hbm.1, f32[3,8,128]{2,1,0:T(8,128)} %bitcast.4, f32[3,8,128]{2,1,0:T(8,128)} %bitcast.5, s32[1,8]{1,0:T(1,128)} %bitcast.6), custom_call_target="tpu_custom_call" | custom-call | tf_op jit(solution)/shard_map/pallas_call | solution.py:673
  21.7 1.1 %shard_map.69 = (f32[19,32,512]{2,1,0:T(8,128)}, f32[3,8,128]{2,1,0:T(8,128)}) custom-call(f32[19,32,512]{2,1,0:T(8,128)S(1)} %get-tuple-element.6.evolved_in, f32[3,8,128]{2,1,0:T(8,128)S(1)} %get-tuple-element.7.moved_in), custom_call_target="tpu_custom_call" | custom-call | tf_op jit(solution)/shard_map/pallas_call | solution.py:723

commit v4 on v3

--- a/solution.py
+++ b/solution.py
@@ -91,8 +91,8 @@
     pop_hbm, wall_hbm, pos_hbm, shift_hbm, home_hbm, fbuf, disp,
     wall, points, home, rbuf, mom, scale, force, vel,
     outgoing, arrived, current, ret_out, ret_in, wxs,
-    xs_out, xs_in, ys_out, ys_in, cs_in,
-    load_sem, out_sem, a2a_recv, ret_recv, halo_send, halo_recv,
+    xs_out, xs_in, ys_out, ys_in, cs_in, meter,
+    load_sem, out_sem, a2a_recv, ret_recv, halo_recv,
 ):
     v = lax.axis_index("vessel")
     h = lax.axis_index("xsec")
@@ -118,17 +118,11 @@
         copy.start()
     load = pltpu.make_async_copy(pop_hbm, fbuf, load_sem.at[2])
     load.start()
-    load_wall = pltpu.make_async_copy(wall_hbm, wall, load_sem.at[3])
+    load_wall = pltpu.make_async_copy(wall_hbm, wall, load_sem.at[2])
     load_wall.start()
+    xs_out[...] = jnp.zeros(xs_out.shape, jnp.float32)
 
     for sy in (1, -1):
-
-        @pl.when(has_side[sy])
-        def _(sy=sy):
-            for sx in (1, -1):
-                pl.semaphore_signal(
-                    barrier, inc=1, device_id=(v_side[sx], h + sy), device_id_type=MESH
-                )
 
         @pl.when(jnp.logical_not(has_side[sy]))
         def _(sy=sy):
@@ -174,8 +168,11 @@
     for o in range(owned):
         place = jnp.where(row == o, homes[o] * capacity + ranks[o], place)
 
-    sides = has_side[1].astype(jnp.int32) + has_side[-1].astype(jnp.int32)
-    pl.semaphore_wait(barrier, n_xsec + 1 + 2 * sides)
+    pl.semaphore_wait(barrier, n_xsec + 1)
+
+    def settle_blocks(ref, i):
+        whole = ref.at[pl.ds(0, n_xsec - 1)]
+        pltpu.make_async_copy(whole, whole, out_sem.at[i]).wait()
 
     def slot_of(sender, receiver):
         return lax.rem(sender - receiver + n_xsec - 1, n_xsec)
@@ -353,8 +350,7 @@
             result.append(current[k, c] + row_sums(parts))
         return result
 
-    load.wait()
-    load_wall.wait()
+    pltpu.make_async_copy(rbuf, rbuf, load_sem.at[2]).wait()
     prepare()
     planes = []
     for k in range(n_xsec):
@@ -366,6 +362,8 @@
         sides, flat = build(0, k, now, [pltpu.roll(now[c], 1, 0) for c in range(3)])
         planes.append(flat)
         add_force(spread(sides, flat), k == 0)
+
+    settle_blocks(outgoing, 0)
 
     depth = lax.broadcasted_iota(jnp.int32, (extent_x, plane), 1) % NZ
     lane = lax.broadcasted_iota(jnp.int32, (extent_x, LANES), 1)
@@ -483,8 +481,8 @@
                     last_tile if sy == 1 else first_tile,
                 ],
                 dst_ref=cs_in.at[it, k],
-                send_sem=halo_send.at[it, 2],
-                recv_sem=halo_recv.at[it, 2],
+                send_sem=out_sem.at[0],
+                recv_sem=halo_recv.at[it],
                 device_id=(v_side[sx], h + sy),
                 device_id_type=MESH,
             )
@@ -498,8 +496,8 @@
             yield None, pltpu.make_async_remote_copy(
                 src_ref=xs_out.at[it, side],
                 dst_ref=xs_in.at[it, side],
-                send_sem=halo_send.at[it, 0],
-                recv_sem=halo_recv.at[it, 0],
+                send_sem=out_sem.at[0],
+                recv_sem=halo_recv.at[it],
                 device_id=(v_side[sx], h),
                 device_id_type=MESH,
             )
@@ -524,31 +522,19 @@
             yield has_side[sy], pltpu.make_async_remote_copy(
                 src_ref=ys_out.at[it, side],
                 dst_ref=ys_in.at[it, side],
-                send_sem=halo_send.at[it, 1],
-                recv_sem=halo_recv.at[it, 1],
+                send_sem=out_sem.at[0],
+                recv_sem=halo_recv.at[it],
                 device_id=(v, h + sy),
                 device_id_type=MESH,
             )
 
-    def settle(it, sent):
-        def wait(kind, ref):
-            copy = pltpu.make_async_remote_copy(
-                src_ref=ref,
-                dst_ref=ref,
-                send_sem=halo_send.at[it, kind],
-                recv_sem=halo_recv.at[it, kind],
-                device_id=(v_side[1], h),
-                device_id_type=MESH,
-            )
-            return copy.wait_send if sent else copy.wait_recv
-
+    def settle(sem):
+        side = row_groups + 1 + len(CORNERS) // 2
         between = jnp.logical_and(has_side[1], has_side[-1])
-        half = len(CORNERS) // 2
-        pl.when(between)(wait(2, cs_in.at[it]))
-        pl.when(jnp.logical_not(between))(wait(2, cs_in.at[it, pl.ds(0, half)]))
-        pl.when(between)(wait(1, ys_in.at[it]))
-        pl.when(jnp.logical_not(between))(wait(1, ys_in.at[it, pl.ds(0, 1)]))
-        wait(0, xs_in.at[it])()
+        most = meter.at[pl.ds(0, 2 * tiles + 2 * side)]
+        some = meter.at[pl.ds(0, 2 * tiles + side)]
+        pl.when(between)(pltpu.make_async_copy(most, most, sem).wait)
+        pl.when(jnp.logical_not(between))(pltpu.make_async_copy(some, some, sem).wait)
 
     def pass_on():
         for q in range(Q):
@@ -592,13 +578,12 @@
             collide(rg, t, it == 0)
         pass_on()
         gather_moments()
-        settle(it, False)
+        settle(halo_recv.at[it])
         values = halo_values(it)
         halo_moments(values)
         find_velocity(last)
         if not last:
             halo_populations(values)
-        if not last:
             built = []
             for k in range(n_xsec):
                 now = move(it, k, planes[k])
@@ -615,7 +600,7 @@
                 ),
                 True,
             )
-            settle(it, True)
+            settle(out_sem.at[0])
 
     for k in range(n_xsec - 1, -1, -1):
         now = move(ITERS - 1, k, planes[k])
@@ -625,6 +610,8 @@
         if k > 0:
             transfer(ret_out.at[k], ret_in, out_sem.at[1], ret_recv, k).start()
     halo_populations(halo_values(ITERS - 1))
+    settle(out_sem.at[0])
+    settle_blocks(ret_out, 1)
     totals = [jnp.zeros((8, LANES), jnp.float32) for _ in range(3)]
     for k in range(n_xsec):
         if k > 0:
@@ -638,10 +625,6 @@
                 totals[c] = jnp.where(here, spread_row(value), totals[c])
     for c in range(3):
         disp[c] = totals[c][0:owned]
-    for i, ref in enumerate((outgoing, ret_out)):
-        whole = ref.at[pl.ds(0, n_xsec - 1)]
-        pltpu.make_async_copy(whole, whole, out_sem.at[i]).wait()
-    settle(ITERS - 1, True)
 
 
 CHUNKS = 1
@@ -667,6 +650,7 @@
     slots = n_xsec * capacity
     extent_x, plane = populations.shape[1:]
     f32 = jnp.float32
+    meters = 2 * (plane // LANES + extent_x // 8 + 1) + len(CORNERS)
     vmem = pl.BlockSpec(memory_space=pltpu.VMEM)
     hbm = pl.BlockSpec(memory_space=pltpu.HBM)
     dma = pltpu.SemaphoreType.DMA
@@ -682,7 +666,7 @@
             pltpu.VMEM((extent_x, plane), jnp.int32),
             pltpu.VMEM((2, 3, owned, LANES), f32),
             pltpu.SMEM((1, owned), jnp.int32),
-            pltpu.VMEM((Q, extent_x, plane), f32),
+            pltpu.VMEM((Q + 1, extent_x, plane), f32),
             pltpu.VMEM((4, extent_x, plane), f32),
             pltpu.VMEM((extent_x, plane), f32),
             pltpu.VMEM((3, extent_x, plane), f32),
@@ -693,17 +677,17 @@
             pltpu.VMEM((n_xsec, 2, 8, LANES), f32),
             pltpu.VMEM((n_xsec, 2, 8, LANES), f32),
             pltpu.VMEM((ITERS, slots, extent_x, LANES), f32),
-            pltpu.VMEM((ITERS, 2, len(X_DIRS[1]), plane), f32),
-            pltpu.VMEM((ITERS, 2, len(X_DIRS[1]), plane), f32),
+            pltpu.VMEM((ITERS, 2, 8, plane), f32),
+            pltpu.VMEM((ITERS, 2, 8, plane), f32),
             pltpu.VMEM((ITERS, 2, extent_x + 8, LANES), f32),
             pltpu.VMEM((ITERS, 2, extent_x + 8, LANES), f32),
             pltpu.VMEM((ITERS, len(CORNERS), 8, LANES), f32),
-            dma((4,)),
+            pltpu.VMEM((meters, 8, LANES), f32),
+            dma((3,)),
             dma((2,)),
             dma((n_xsec - 1,)),
             dma((n_xsec - 1,)),
-            dma((ITERS, 3)),
-            dma((ITERS, 3)),
+            dma((ITERS,)),
         ],
         compiler_params=pltpu.CompilerParams(
             collective_id=0, has_side_effects=True, vmem_limit_bytes=40 << 20

time: 23 us -> 22.8 us (level)
  no operation moved by 1% of the time
where the time goes in v4:
time: 22.8 us; the launch traced here: 22.6 us
  Pallas kernels  21.9 us (96%)
  between operations  0.64 us (3%)
    pallas_call x1, Pallas kernels, per_device(): pl.pallas_call(functools.partial(kernel, n_vessel, n_xsec, capacity, exte...  20.9 us
    pallas_call x1, Pallas kernels, per_device(): pl.pallas_call(hand_over, out_shape=(jax.ShapeDtypeStruct(evolved.shape,...  1.06 us

profile of v4, /device:TPU:0, one launch (start us, length us, event | category | flops | bytes accessed | tf_op | source)
XLA Modules:
  0.0 22.6 jit_solution(6004100537861632401)
XLA Ops:
  0.6 20.9 %shard_map.68 = (f32[19,32,512]{2,1,0:T(8,128)S(1)}, f32[3,8,128]{2,1,0:T(8,128)S(1)}) custom-call(f32[19,32,512]{2,1,0:T(8,128)} %pop_hbm.1, s32[32,512]{1,0:T(8,128)} %wall_hbm.1, f32[3,8,128]{2,1,0:T(8,128)} %bitcast.4, f32[3,8,128]{2,1,0:T(8,128)} %bitcast.5, s32[1,8]{1,0:T(1,128)} %bitcast.6), custom_call_target="tpu_custom_call" | custom-call | tf_op jit(solution)/shard_map/pallas_call | solution.py:657
  21.5 1.1 %shard_map.69 = (f32[19,32,512]{2,1,0:T(8,128)}, f32[3,8,128]{2,1,0:T(8,128)}) custom-call(f32[19,32,512]{2,1,0:T(8,128)S(1)} %get-tuple-element.6.evolved_in, f32[3,8,128]{2,1,0:T(8,128)S(1)} %get-tuple-element.7.moved_in), custom_call_target="tpu_custom_call" | custom-call | tf_op jit(solution)/shard_map/pallas_call | solution.py:707

commit v5 on v4

--- a/solution.py
+++ b/solution.py
@@ -116,10 +116,6 @@
     ]
     for copy in small_loads:
         copy.start()
-    load = pltpu.make_async_copy(pop_hbm, fbuf, load_sem.at[2])
-    load.start()
-    load_wall = pltpu.make_async_copy(wall_hbm, wall, load_sem.at[2])
-    load_wall.start()
     xs_out[...] = jnp.zeros(xs_out.shape, jnp.float32)
 
     for sy in (1, -1):
@@ -135,6 +131,10 @@
 
     pltpu.make_async_copy(points, points, load_sem.at[0]).wait()
     small_loads[2].wait()
+    load = pltpu.make_async_copy(pop_hbm, fbuf, load_sem.at[2])
+    load.start()
+    load_wall = pltpu.make_async_copy(wall_hbm, wall, load_sem.at[2])
+    load_wall.start()
 
     row = lax.broadcasted_iota(jnp.int32, (8, LANES), 0)
     odd_row = (row & 1) == 1

time: 22.8 us -> 22.8 us (level)
  no operation moved by 1% of the time
where the time goes in v5:
time: 22.8 us; the launch traced here: 22.6 us
  Pallas kernels  21.9 us (96%)
  between operations  0.64 us (3%)
    pallas_call x1, Pallas kernels, per_device(): pl.pallas_call(functools.partial(kernel, n_vessel, n_xsec, capacity, exte...  20.9 us
    pallas_call x1, Pallas kernels, per_device(): pl.pallas_call(hand_over, out_shape=(jax.ShapeDtypeStruct(evolved.shape,...  1.06 us

profile of v5, /device:TPU:0, one launch (start us, length us, event | category | flops | bytes accessed | tf_op | source)
XLA Modules:
  0.0 22.6 jit_solution(339680720886504362)
XLA Ops:
  0.6 20.9 %shard_map.68 = (f32[19,32,512]{2,1,0:T(8,128)S(1)}, f32[3,8,128]{2,1,0:T(8,128)S(1)}) custom-call(f32[19,32,512]{2,1,0:T(8,128)} %pop_hbm.1, s32[32,512]{1,0:T(8,128)} %wall_hbm.1, f32[3,8,128]{2,1,0:T(8,128)} %bitcast.4, f32[3,8,128]{2,1,0:T(8,128)} %bitcast.5, s32[1,8]{1,0:T(1,128)} %bitcast.6), custom_call_target="tpu_custom_call" | custom-call | tf_op jit(solution)/shard_map/pallas_call | solution.py:657
  21.5 1.1 %shard_map.69 = (f32[19,32,512]{2,1,0:T(8,128)}, f32[3,8,128]{2,1,0:T(8,128)}) custom-call(f32[19,32,512]{2,1,0:T(8,128)S(1)} %get-tuple-element.6.evolved_in, f32[3,8,128]{2,1,0:T(8,128)S(1)} %get-tuple-element.7.moved_in), custom_call_target="tpu_custom_call" | custom-call | tf_op jit(solution)/shard_map/pallas_call | solution.py:707
